TPU v7x, 32 devices: a whole 2x2x4 slice. The times are simulated.
32 devices in a mesh: groups: 2 (over y), seq: 4 (over z), section: 4 (over x, core).
Axes of the slice: x: 2, y: 2, z: 4, core: 2. Of those that a mesh axis runs over, the one named last changes fastest.
Arguments:
- hidden: bfloat16 [4, 32, 3072], P('section', ('groups', 'seq')), parts along dimension 1, may hold values from -6 to 6
- kv_cache: bfloat16 [4, 4, 32, 2, 3072], P('section', None, ('groups', 'seq')), parts along dimension 2, may hold values from -400 to 400
- w_qkv: bfloat16 [4, 3072, 3, 3072], P('section', None, None, 'seq'), may hold values from -0.109375 to 0.109375
- w_out: bfloat16 [4, 3072, 3072], P('section', None, 'seq'), may hold values from -0.109375 to 0.109375
- norm_gain: float32 [4, 2, 128], P('section'), may hold values from 1 to 2
- modulation: float32 [4, 4, 3, 3072], P('section'), may hold values from -5 to 5
- patch_order: int32 [8], P('groups'), parts along dimension 0, may hold values from 0 to 3, each once
- timestep: int32 [8], P('groups'), parts along dimension 0, may hold values from 0 to 3
Outputs:
- next_hidden: bfloat16 [4, 32, 3072], P('section', ('groups', 'seq')), parts along dimension 1
- fresh_kv: bfloat16 [4, 32, 2, 3072], P('section', ('groups', 'seq')), parts along dimension 1
There are 2 independent parts, one for each index of `groups`. A program takes and returns all parts, laid end to end along the dimension named above; an argument that names none is the same for every part. Nothing has to cross between parts.
Inputs may be any that keep to these rules, and one draw needn't show every extreme that they name: `patch_order`: each section holds a different patch.
All inputs are finite; a program needn't handle non-finite values.
Results may differ from a plain program's by a relative error of at most 0.02.
The roundings to bfloat16 on the way count: a program that leaves them out, or rounds other values in their place, can miss the bound.
Values may be sent and summed in bfloat16 or wider, within the bound.
No kernel may reach another device: no remote copies, remote signals or barrier semaphores. Data moves between devices by JAX's collectives and lax.ppermute only.
A program may use at most 64 MiB of HBM per device.

v0:
```python
import functools
import math

import jax
import jax.numpy as jnp
from jax import lax
from jax.experimental import pallas as pl
from jax.experimental.pallas import tpu as pltpu
from jax.sharding import PartitionSpec as P


APART = (1, 2)
TURNS = ((3, 2), (0, 3), (2, 1), (1, 0))

F32 = jnp.float32
BF16 = jnp.bfloat16
VMEM = pl.BlockSpec(memory_space=pltpu.VMEM)


def passed_along(array, axis, by):
    count = lax.axis_size(axis)
    return lax.ppermute(array, axis, [(i, (i + by) % count) for i in range(count)])


def layer_norm(values_in):
    center = values_in - jnp.mean(values_in, axis=-1, keepdims=True)
    spread = jnp.mean(center * center, axis=-1, keepdims=True)
    return center * lax.rsqrt(spread + 1e-06)


def head_norm(values_in, gain):
    square = jnp.mean(values_in * values_in, axis=-1, keepdims=True)
    return values_in * lax.rsqrt(square + 1e-06) * gain


def swapped(slots, number):
    return jnp.concatenate([slots[b ^ number] for b in range(len(slots))], axis=0)


def ahead_kernel(out_ref):
    out_ref[...] = jnp.zeros_like(out_ref)


def entry(ref):
    lane = lax.broadcasted_iota(jnp.int32, ref.shape, 1)
    mine = lane == lax.axis_index("section")
    return jnp.sum(jnp.where(mine, ref[...], 0).astype(F32), axis=1, keepdims=True)


def pack_kernel(order_ref, _, hidden_ref, cache_ref, *outs, numbers, slots, patches, columns, split):
    mine = lax.axis_index("seq")
    patch = entry(order_ref)
    for out, b in zip(outs, numbers, strict=True):
        start = pl.multiple_of((mine ^ b) * columns, columns)
        both = [cache_ref[0, p, :, :, pl.ds(start, columns)].astype(F32) for p in range(patches)]
        both = [x[:, part] for part in range(2) for x in both]
        stale = []
        for part in range(2):
            for i in range(part * patches, (part + 1) * patches - 1):
                stale.append(jnp.where(patch > i - part * patches, both[i], both[i + 1]))
        stale = jnp.concatenate(stale, axis=0).astype(BF16)
        out[: stale.shape[0]] = stale
        if b and b not in split:
            hidden = hidden_ref[...].astype(F32)
            hidden = [hidden[:, c * columns : (c + 1) * columns] for c in range(slots)]
            out[stale.shape[0] :] = jnp.concatenate(hidden, axis=0).astype(BF16)


def project_kernel(step_ref, mod_ref, gain_ref, weight_ref, *refs, slots, tokens, heads, size, stale):
    hidden_refs = refs[:slots][::-1]
    q_ref, k_ref, normed_ref, held_ref, gate_ref, scratch = refs[slots:]
    mine = lax.axis_index("seq")
    columns, length = heads * size, slots * tokens
    step = lax.broadcasted_iota(jnp.int32, (mod_ref.shape[1], 1), 0).astype(F32) == entry(step_ref)
    modulate = [jnp.sum(jnp.where(step, mod_ref[i], 0.0), axis=0, keepdims=True) for i in range(2)]
    start = pl.multiple_of(mine * columns, columns)
    rows = []
    for ref in hidden_refs:
        if ref.shape[0] == tokens:
            rows.append(ref[...].astype(F32))
        else:
            cut = ref[2 * stale :].astype(F32)
            rows.append(jnp.concatenate([cut[c * tokens : (c + 1) * tokens] for c in range(slots)], axis=1))
    rows = jnp.concatenate(rows, axis=0)
    normed = (layer_norm(rows) * (1.0 + modulate[1]) + modulate[0]).astype(BF16)
    normed_ref[...] = normed
    for part, out in enumerate((q_ref, k_ref)):
        dotted = jnp.dot(normed, weight_ref[part], preferred_element_type=F32).astype(BF16).astype(F32)
        stacked = jnp.concatenate([dotted[:, h * size : (h + 1) * size] for h in range(heads)], axis=0)
        stacked = head_norm(stacked, gain_ref[pl.ds(part, 1), :]).astype(BF16)
        for h in range(heads):
            out[:, h * size : (h + 1) * size] = stacked[h * length : (h + 1) * length]
    scratch[...] = rows
    held_ref[...] = scratch[:, pl.ds(start, columns)].astype(BF16)
    gates = jnp.where(step, mod_ref[2, :, pl.ds(start, columns)], 0.0)
    gate_ref[...] = jnp.sum(gates, axis=0, keepdims=True)


def attend_kernel(q_ref, k_ref, normed_ref, weight_ref, *refs, slots, tokens, stale, heads, size):
    old, outs = refs[:slots][::-1], refs[slots:]
    old = [r[: 2 * stale].astype(F32) for r in old]
    fresh_keys = k_ref[...].astype(F32)
    own = [slice(b * tokens, (b + 1) * tokens) for b in range(slots)]
    per = stale + tokens
    count = slots * per
    keys = jnp.concatenate([x for b in range(slots) for x in (old[b][:stale], fresh_keys[own[b]])], axis=0).astype(BF16)
    queries = q_ref[...]
    length = queries.shape[0]
    cuts = [slice(h * size, (h + 1) * size) for h in range(heads)]
    dims = (((1,), (1,)), ((), ()))
    scores = [lax.dot_general(queries[:, cut], keys[:, cut], dims, preferred_element_type=F32) for cut in cuts]
    fresh_values = jnp.dot(normed_ref[...], weight_ref[2], preferred_element_type=F32).astype(BF16).astype(F32)
    scores = jnp.concatenate(scores, axis=0) / math.sqrt(size)
    top = jnp.max(scores, axis=-1, keepdims=True)
    weights = jnp.exp(scores - top).astype(BF16).astype(F32)
    values = [x for b in range(slots) for x in (old[b][stale:], fresh_values[own[b]])]
    values = jnp.concatenate(values, axis=0).astype(BF16)
    lane = lax.broadcasted_iota(jnp.int32, weights.shape, 1)
    apart = [jnp.where((lane >= b * per) & (lane < (b + 1) * per), weights, 0.0).astype(BF16) for b in range(slots)]
    ones = jnp.ones((count, size), BF16)
    sums = []
    for h, cut in enumerate(cuts):
        rows = jnp.concatenate([x[h * length : (h + 1) * length] for x in apart], axis=0)
        extended = jnp.concatenate([values[:, cut], ones], axis=1)
        sums.append(jnp.dot(rows, extended, preferred_element_type=F32))
    rows = []
    for both in sums:
        both = both.astype(BF16).astype(F32)
        total = both[:length]
        for b in range(1, slots):
            total = total + both[b * length : (b + 1) * length]
        rows.append(total[:, :size] / total[:, size:])
    rows = jnp.concatenate(rows, axis=1)
    pieces = [rows[b * tokens : (b + 1) * tokens] for b in range(slots)]
    for b in range(slots):
        outs[b][:length] = swapped(pieces, b).astype(BF16)
        outs[b][length:] = jnp.concatenate([fresh_keys[own[b]], fresh_values[own[b]]], axis=0).astype(BF16)


def partial_kernel(weight_ref, *refs, numbers, rows, before):
    columns = weight_ref.shape[1]
    mine = lax.axis_index("seq")
    total = refs[len(numbers)][...] if before else None
    for ref, b in zip(refs[: len(numbers)], numbers, strict=True):
        start = pl.multiple_of((mine ^ b) * columns, columns)
        term = jnp.dot(ref[:rows], weight_ref[pl.ds(start, columns), :], preferred_element_type=F32)
        total = term if total is None else total + term
    refs[-1][...] = total


def output_kernel(gate_ref, held_ref, weight_ref, total_ref, attention_ref, *outs, number, tokens, turns):
    columns = weight_ref.shape[1]
    start = pl.multiple_of((lax.axis_index("seq") ^ number) * columns, columns)
    rows = total_ref.shape[0]
    total = total_ref[...] + jnp.dot(
        attention_ref[:rows], weight_ref[pl.ds(start, columns), :], preferred_element_type=F32
    )
    block = held_ref[...].astype(F32) + gate_ref[...] * total.astype(BF16).astype(F32)
    pieces = [block[b * tokens : (b + 1) * tokens] for b in range(len(outs))]
    even = lax.rem(lax.axis_index("section"), 2) == 0
    for out, (b, c) in zip(outs, turns, strict=True):
        out[...] = jnp.where(even, pieces[b], pieces[c]).astype(BF16)


def place_kernel(*refs, slots, turns):
    out_ref, refs = refs[slots], refs[:slots][::-1]
    columns = refs[0].shape[1]
    mine, sections = lax.axis_index("seq"), lax.axis_size("section")
    even = lax.rem(lax.axis_index("section") + (sections - 1), sections) % 2 == 0
    for ref, (b, c) in zip(refs, turns, strict=True):
        start = pl.multiple_of((mine ^ jnp.where(even, b, c)) * columns, columns)
        out_ref[0, :, pl.ds(start, columns)] = ref[...]


def place_kv_kernel(*refs, slots, tokens):
    out_ref, refs = refs[slots], refs[:slots][::-1]
    columns = refs[0].shape[1]
    mine = lax.axis_index("seq")
    for b in range(slots):
        start = pl.multiple_of((mine ^ b) * columns, columns)
        piece = refs[b][slots * tokens :].astype(F32)
        both = jnp.stack([piece[:tokens], piece[tokens:]], axis=1)
        out_ref[0, :, :, pl.ds(start, columns)] = both.astype(BF16)


def call(kernel, flops, out_shape, operands, scratch=(), **sizes):
    return pl.pallas_call(
        functools.partial(kernel, **sizes),
        out_shape=out_shape,
        in_specs=[VMEM] * len(operands),
        out_specs=jax.tree.map(lambda _: VMEM, out_shape),
        scratch_shapes=scratch,
        compiler_params=pltpu.CompilerParams(vmem_limit_bytes=16 * 2**20),
        cost_estimate=pl.CostEstimate(flops=int(flops), transcendentals=0, bytes_accessed=2**20),
    )(*operands)


def apart(slots):
    return APART if slots > 2 else ()


def body_by_heads(hidden, kv_cache, w_qkv, w_out, norm_gain, modulation, patch_order, timestep):
    slots, sections = lax.axis_size("seq"), lax.axis_size("section")
    tokens, width = hidden.shape[1:]
    patches = kv_cache.shape[1]
    columns, size = w_qkv.shape[3], norm_gain.shape[2]
    heads, stale, rows = columns // size, (patches - 1) * tokens, slots * tokens
    split = apart(slots)
    turns = TURNS if slots == 4 else [(b, b) for b in range(slots)]

    def array(*shape, dtype=BF16):
        return jax.ShapeDtypeStruct(shape, dtype)

    def moved(array, number):
        return lax.ppermute(array, "seq", [(j, j ^ number) for j in range(slots)])

    def onward(array, turn):
        pairs = [
            (j * sections + s, (j ^ turn[s % 2]) * sections + (s + 1) % sections)
            for j in range(slots)
            for s in range(sections)
        ]
        return lax.ppermute(array, ("seq", "section"), pairs)

    def exchanged(arrays):
        return [arrays[0]] + [moved(arrays[b], b) for b in range(1, slots)]

    own = hidden[0]
    alone = {b: moved(own, b) for b in split}
    ahead = call(ahead_kernel, 5e9, array(8, 128, dtype=F32), [])
    packed = {}
    far = tuple(b for b in range(1, slots) if b not in split)
    for numbers in (far, (0, *split)):
        outs = call(
            pack_kernel,
            5e9,
            [array(2 * stale + (rows if b in far else 0), columns) for b in numbers],
            [patch_order[None], ahead, own, kv_cache],
            numbers=numbers,
            slots=slots,
            patches=patches,
            columns=columns,
            split=split,
        )
        packed |= dict(zip(numbers, outs, strict=True))
    packed = [packed[b] for b in range(slots)]
    old = exchanged(packed)
    inputs = [own] + [alone[b] if b in split else old[b] for b in range(1, slots)]
    weights = jnp.transpose(w_qkv[0], (1, 0, 2))
    queries, keys, normed, held, gate = call(
        project_kernel,
        2e9,
        [
            array(rows, columns),
            array(rows, columns),
            array(rows, width),
            array(rows, columns),
            array(1, columns, dtype=F32),
        ],
        [timestep[None], jnp.transpose(modulation[0], (1, 0, 2)), norm_gain[0], weights, *inputs[::-1]],
        scratch=[pltpu.VMEM((rows, width), F32)],
        slots=slots,
        tokens=tokens,
        heads=heads,
        size=size,
        stale=stale,
    )
    ordered = call(
        attend_kernel,
        2e9,
        [array(rows + 2 * tokens, columns)] * slots,
        [queries, keys, normed, weights, *old[::-1]],
        slots=slots,
        tokens=tokens,
        stale=stale,
        heads=heads,
        size=size,
    )
    attention = exchanged(ordered)
    out_weights = w_out[0]
    groups = [(0, 2), (3,)]
    total = []
    for numbers in groups:
        operands = [out_weights] + [attention[b] for b in numbers] + total
        total = [
            call(
                partial_kernel,
                1e9,
                array(rows, columns, dtype=F32),
                operands,
                numbers=numbers,
                rows=rows,
                before=bool(total),
            )
        ]
    pieces = call(
        output_kernel,
        2e9,
        [array(tokens, columns)] * slots,
        [gate, held, out_weights, *total, attention[1]],
        number=1,
        tokens=tokens,
        turns=turns,
    )
    arrived = [onward(piece, turn) for piece, turn in zip(pieces, turns, strict=True)]
    fresh_kv = call(place_kv_kernel, 1e9, array(1, tokens, 2, width), attention[::-1], slots=slots, tokens=tokens)
    next_hidden = call(place_kernel, 1e9, array(1, tokens, width), arrived[::-1], slots=slots, turns=turns)
    return (next_hidden, fresh_kv)


def body_by_tokens(hidden, kv_cache, w_qkv, w_out, norm_gain, modulation, patch_order, timestep):
    section_index = lax.axis_index("section")
    patch_index = lax.dynamic_index_in_dim(patch_order, section_index, 0, keepdims=False)
    step_index = lax.dynamic_index_in_dim(timestep, section_index, 0, keepdims=False)
    modulate = lax.dynamic_index_in_dim(modulation[0], step_index, 0, keepdims=False)
    model_width = hidden.shape[2]
    head_size = norm_gain.shape[2]
    head_count = model_width // head_size
    col_width = w_qkv.shape[3]
    rows_in = hidden[0].astype(jnp.float32)
    own_count = rows_in.shape[0]
    normed = (layer_norm(rows_in) * (1.0 + modulate[1]) + modulate[0]).astype(jnp.bfloat16)
    w_local = w_qkv[0].reshape(model_width, 3 * col_width)
    projected = jnp.dot(
        lax.all_gather(normed, "seq", axis=0, tiled=True),
        w_local,
        preferred_element_type=jnp.float32,
    ).astype(jnp.bfloat16)
    patch_len = projected.shape[0]
    projected = projected.reshape(patch_len, 3, col_width)
    query_cols = lax.all_gather(projected[:, 0], "seq", axis=1, tiled=True)
    kv_rows = lax.all_to_all(projected[:, 1:], "seq", split_axis=0, concat_axis=2, tiled=True)
    queries = head_norm(
        query_cols.astype(jnp.float32).reshape(patch_len, head_count, head_size), norm_gain[0, 0]
    ).astype(jnp.bfloat16)
    key_rows = head_norm(
        kv_rows[:, 0].astype(jnp.float32).reshape(own_count, head_count, head_size), norm_gain[0, 1]
    ).astype(jnp.bfloat16)
    fresh = jnp.stack([key_rows.reshape(own_count, model_width), kv_rows[:, 1]], axis=1)
    zero = jnp.zeros((), jnp.int32)
    local_kv = lax.dynamic_update_slice(kv_cache[0], fresh[None], (patch_index, zero, zero, zero))
    patch_count = local_kv.shape[0]
    local_keys = local_kv[:, :, 0].reshape(patch_count * own_count, head_count, head_size)
    local_values = local_kv[:, :, 1].reshape(patch_count * own_count, head_count, head_size)
    scores = jnp.einsum(
        "thd,shd->hts", queries, local_keys, preferred_element_type=jnp.float32
    ) / math.sqrt(head_size)
    row_top = lax.pmax(jnp.max(scores, axis=-1), "seq")
    weights = jnp.exp(scores - row_top[:, :, None]).astype(jnp.bfloat16)
    denominator = jnp.sum(weights, axis=-1, dtype=jnp.float32).T
    numerator = jnp.einsum(
        "hts,shd->thd", weights, local_values, preferred_element_type=jnp.float32
    ).reshape(patch_len, model_width)
    totals, counts = (
        lax.psum(numerator.astype(jnp.bfloat16), "seq").astype(jnp.float32),
        lax.psum(denominator.astype(jnp.bfloat16), "seq").astype(jnp.float32),
    )
    attention = (totals.reshape(patch_len, head_count, head_size) / counts[:, :, None]).astype(
        jnp.bfloat16
    )
    attention = attention.reshape(patch_len, model_width)
    out_cols = jnp.dot(attention, w_out[0], preferred_element_type=jnp.float32).astype(jnp.bfloat16)
    out_rows = lax.all_to_all(out_cols, "seq", split_axis=0, concat_axis=1, tiled=True)
    block = (rows_in + modulate[2] * out_rows.astype(jnp.float32)).astype(jnp.bfloat16)
    arrived = passed_along(block, "section", 1)
    return (arrived[None], fresh[None])


def body(hidden, kv_cache, w_qkv, w_out, norm_gain, modulation, patch_order, timestep):
    count = lax.axis_size("seq")
    whole_heads = w_qkv.shape[3] % norm_gain.shape[2] == 0
    chosen = body_by_heads if whole_heads and count & (count - 1) == 0 else body_by_tokens
    return chosen(hidden, kv_cache, w_qkv, w_out, norm_gain, modulation, patch_order, timestep)


def solution(mesh):
    return jax.shard_map(
        body,
        mesh=mesh,
        in_specs=(
            P("section", ("groups", "seq"), None),
            P("section", None, ("groups", "seq"), None, None),
            P("section", None, None, "seq"),
            P("section", None, "seq"),
            P("section", None, None),
            P("section", None, None, None),
            P("groups"),
            P("groups"),
        ),
        out_specs=(
            P("section", ("groups", "seq"), None),
            P("section", ("groups", "seq"), None, None),
        ),
        check_vma=False,
    )
```

profile of v0, /device:TPU:1, one launch (start us, length us, event | category | flops | bytes accessed | tf_op | source)
XLA Modules:
  0.0 32.4 jit_solution(17688302355253026467)
XLA Ops:
  0.6 0.0 copy-start.1
  0.6 0.0 copy-start.5
  0.6 0.0 copy-start.4
  0.7 3.2 %collective-permute-start.1 = (bf16[4,3072]{1,0:T(4,128)(2,1)}, bf16[4,3072]{1,0:T(4,128)(2,1)S(1)}, u32[]{:S(2)}, u32[]{:S(2)}) collective-permute-start(bf16[4,3072]{1,0:T(4,128)(2,1)} %bitcast.21), channel_id=1, source_target_pairs={{0,8},{4,12},{8,0},{12,4},{1,9},{5,13},{9,1},{13,5},{2,10},{6,14},... | collective-permute-start | bytes 73736 | tf_op jit(solution)/shard_map/ppermute | solution.py:215
  3.9 1.3 %collective-permute-start.2 = (bf16[4,3072]{1,0:T(4,128)(2,1)}, bf16[4,3072]{1,0:T(4,128)(2,1)S(1)}, u32[]{:S(2)}, u32[]{:S(2)}) collective-permute-start(bf16[4,3072]{1,0:T(4,128)(2,1)} %bitcast.22), channel_id=1, source_target_pairs={{0,4},{4,0},{8,12},{12,8},{1,5},{5,1},{9,13},{13,9},{2,6},{6,2},{1... | collective-permute-start | bytes 73736 | tf_op jit(solution)/shard_map/ppermute | solution.py:215
  5.2 0.0 copy-done.4
  5.2 0.0 slice-start
  5.2 0.0 slice-start.1
  5.2 0.0 copy-start
  5.2 0.0 copy-start.2
  5.2 0.0 copy-start.3
  5.2 0.1 shard_map.96
  5.3 0.0 slice-start.2
  5.4 0.0 slice-start.3
  5.4 0.6 %collective-permute-start = (bf16[40,768]{1,0:T(8,128)(2,1)S(1)}, bf16[40,768]{1,0:T(8,128)(2,1)S(1)}, u32[]{:S(2)}, u32[]{:S(2)}) collective-permute-start(bf16[40,768]{1,0:T(8,128)(2,1)S(1)} %shard_map.96), channel_id=1, source_target_pairs={{0,12},{4,8},{8,4},{12,0},{1,13},{5,9},{9,5},{13,1},{2,14},{6,10},... | collective-permute-start | bytes 184328 | tf_op jit(solution)/shard_map/ppermute | solution.py:215
  6.0 0.2 shard_map.98
  6.2 0.9 %collective-permute-start.3 = (bf16[24,768]{1,0:T(8,128)(2,1)S(1)}, bf16[24,768]{1,0:T(8,128)(2,1)S(1)}, u32[]{:S(2)}, u32[]{:S(2)}) collective-permute-start(bf16[24,768]{1,0:T(8,128)(2,1)S(1)} %get-tuple-element.23), channel_id=1, source_target_pairs={{0,8},{4,12},{8,0},{12,4},{1,9},{5,13},{9,1},{13,5},{2,10},{6,14},... | collective-permute-start | bytes 110600 | tf_op jit(solution)/shard_map/ppermute | solution.py:215
  7.0 2.2 %collective-permute-start.4 = (bf16[24,768]{1,0:T(8,128)(2,1)S(1)}, bf16[24,768]{1,0:T(8,128)(2,1)S(1)}, u32[]{:S(2)}, u32[]{:S(2)}) collective-permute-start(bf16[24,768]{1,0:T(8,128)(2,1)S(1)} %get-tuple-element.24), channel_id=1, source_target_pairs={{0,4},{4,0},{8,12},{12,8},{1,5},{5,1},{9,13},{13,9},{2,6},{6,2},{1... | collective-permute-start | bytes 110600 | tf_op jit(solution)/shard_map/ppermute | solution.py:215
  9.2 0.0 collective-permute-done.1.refs_1_
  9.2 0.0 collective-permute-done.2.refs_2_
  9.2 1.2 %collective-permute-done.refs_0_ = bf16[40,768]{1,0:T(8,128)(2,1)S(1)} collective-permute-done((bf16[40,768]{1,0:T(8,128)(2,1)S(1)}, bf16[40,768]{1,0:T(8,128)(2,1)S(1)}, u32[]{:S(2)}, u32[]{:S(2)}) %collective-permute-start) | collective-permute-done | bytes 61472 | tf_op jit(solution)/shard_map/ppermute | solution.py:215
  10.4 0.0 slice-done
  10.4 0.0 copy-done
  10.5 0.0 slice-start.4
  10.5 1.6 %shard_map.97 = (bf16[16,768]{1,0:T(8,128)(2,1)S(1)}, bf16[16,768]{1,0:T(8,128)(2,1)S(1)}, bf16[16,3072]{1,0:T(8,128)(2,1)S(1)}, bf16[16,768]{1,0:T(8,128)(2,1)S(1)}, f32[1,768]{1,0:T(1,128)S(1)}) custom-call(s32[1,4]{1,0:T(1,128)S(1)} %bitcast.27, f32[3,4,3072]{2,1,0:T(4,128)S(1)} %bitcast.20, f32[2,128]{1,0:T(2,128)S(1)} %bitcast.26, ...), custom_call_target="tpu_custom_call" | custom-call | flops 2000000000 | bytes 1048576 | tf_op jit(solution)/shard_map/pallas_call | solution.py:187
  12.2 0.0 collective-permute-done.3.refs_1_
  12.2 0.0 collective-permute-done.4.refs_2_
  12.2 0.0 slice-start.5
  12.2 1.0 %shard_map.99 = (bf16[24,768]{1,0:T(8,128)(2,1)S(1)}, bf16[24,768]{1,0:T(8,128)(2,1)S(1)}, bf16[24,768]{1,0:T(8,128)(2,1)S(1)}, bf16[24,768]{1,0:T(8,128)(2,1)S(1)}) custom-call(bf16[16,768]{1,0:T(8,128)(2,1)S(1)} %get-tuple-element.20.q_ref, bf16[16,768]{1,0:T(8,128)(2,1)S(1)} %get-tuple-element.21.k_ref, ...), custom_call_target="tpu_custom_call" | custom-call | flops 2000000000 | bytes 1048576 | tf_op jit(solution)/shard_map/pallas_call | solution.py:187
  13.2 0.1 collective-permute-start.6
  13.3 2.4 %collective-permute-start.5 = (bf16[24,768]{1,0:T(8,128)(2,1)S(1)}, bf16[24,768]{1,0:T(8,128)(2,1)S(1)}, u32[]{:S(2)}, u32[]{:S(2)}) collective-permute-start(bf16[24,768]{1,0:T(8,128)(2,1)S(1)} %get-tuple-element.26), channel_id=1, source_target_pairs={{0,12},{4,8},{8,4},{12,0},{1,13},{5,9},{9,5},{13,1},{2,14},{6,10},... | collective-permute-start | bytes 110600 | tf_op jit(solution)/shard_map/ppermute | solution.py:215
  15.7 0.2 collective-permute-start.7
  15.9 1.5 %collective-permute-done.6.refs_1_ = bf16[24,768]{1,0:T(8,128)(2,1)S(1)} collective-permute-done((bf16[24,768]{1,0:T(8,128)(2,1)S(1)}, bf16[24,768]{1,0:T(8,128)(2,1)S(1)}, u32[]{:S(2)}, u32[]{:S(2)}) %collective-permute-start.6) | collective-permute-done | bytes 36896 | tf_op jit(solution)/shard_map/ppermute | solution.py:215
  17.4 0.4 %shard_map.100.refs_1_ = f32[16,768]{1,0:T(8,128)S(1)} custom-call(bf16[3072,768]{1,0:T(8,128)(2,1)S(1)} %bitcast.17, bf16[24,768]{1,0:T(8,128)(2,1)S(1)} %get-tuple-element.27.refs_0_.refs_3_, bf16[24,768]{1,0:T(8,128)(2,1)S(1)} %collective-permute-done.6.refs_1_), custom_call_target="tpu_custom_call" | custom-call | flops 1000000000 | bytes 1048576 | tf_op jit(solution)/shard_map/pallas_call | solution.py:187
  17.8 0.2 collective-permute-done.5.refs_0_
  18.0 0.3 shard_map.101.total_ref
  18.2 0.3 collective-permute-done.7.attention_ref.refs_2_
  18.5 0.3 shard_map.102
  18.8 5.7 %collective-permute-start.8 = (bf16[4,768]{1,0:T(4,128)(2,1)S(1)}, bf16[4,768]{1,0:T(4,128)(2,1)S(1)}, u32[]{:S(2)}, u32[]{:S(2)}) collective-permute-start(bf16[4,768]{1,0:T(4,128)(2,1)S(1)} %get-tuple-element.30), channel_id=1, source_target_pairs={{0,5},{1,2},{2,7},{3,0},{4,1},{5,6},{6,3},{7,4},{8,13},{9,10},{10,... | collective-permute-start | bytes 18440 | tf_op jit(solution)/shard_map/ppermute | solution.py:223
  24.4 0.0 collective-permute-start.9
  24.5 2.4 %collective-permute-start.10 = (bf16[4,768]{1,0:T(4,128)(2,1)S(1)}, bf16[4,768]{1,0:T(4,128)(2,1)S(1)}, u32[]{:S(2)}, u32[]{:S(2)}) collective-permute-start(bf16[4,768]{1,0:T(4,128)(2,1)S(1)} %get-tuple-element.32), channel_id=1, source_target_pairs={{0,1},{1,14},{2,3},{3,12},{4,5},{5,10},{6,7},{7,8},{8,9},{9,6},{10... | collective-permute-start | bytes 18440 | tf_op jit(solution)/shard_map/ppermute | solution.py:223
  26.9 0.2 collective-permute-start.11
  27.1 0.7 %shard_map.104 = bf16[1,4,2,3072]{3,2,1,0:T(2,128)(2,1)} custom-call(bf16[24,768]{1,0:T(8,128)(2,1)S(1)} %collective-permute-done.5.refs_0_, bf16[24,768]{1,0:T(8,128)(2,1)S(1)} %collective-permute-done.6.refs_1_, bf16[24,768]{1,0:T(8,128)(2,1)S(1)} %collective-permute-done.7.attention_ref.refs_2_, bf16[24,768]{1,0:T(8,128)(2,1)S(1)} %get-tuple-element.27.refs_0_.refs_3_), custom_call_target="tpu_custom_call" | custom-call | flops 1000000000 | bytes 1048576 | tf_op jit(solution)/shard_map/pallas_call | solution.py:187
  27.8 0.0 collective-permute-done.8.refs_0_
  27.8 0.6 %collective-permute-done.9.refs_1_ = bf16[4,768]{1,0:T(4,128)(2,1)S(1)} collective-permute-done((bf16[4,768]{1,0:T(4,128)(2,1)S(1)}, bf16[4,768]{1,0:T(4,128)(2,1)S(1)}, u32[]{:S(2)}, u32[]{:S(2)}) %collective-permute-start.9) | collective-permute-done | bytes 6176 | tf_op jit(solution)/shard_map/ppermute | solution.py:223
  28.4 0.0 collective-permute-done.10.refs_2_
  28.4 3.3 %collective-permute-done.11.refs_3_ = bf16[4,768]{1,0:T(4,128)(2,1)S(1)} collective-permute-done((bf16[4,768]{1,0:T(4,128)(2,1)S(1)}, bf16[4,768]{1,0:T(4,128)(2,1)S(1)}, u32[]{:S(2)}, u32[]{:S(2)}) %collective-permute-start.11) | collective-permute-done | bytes 6176 | tf_op jit(solution)/shard_map/ppermute | solution.py:223
  31.7 0.6 %shard_map.103 = bf16[1,4,3072]{2,1,0:T(4,128)(2,1)} custom-call(bf16[4,768]{1,0:T(4,128)(2,1)S(1)} %collective-permute-done.8.refs_0_, bf16[4,768]{1,0:T(4,128)(2,1)S(1)} %collective-permute-done.9.refs_1_, bf16[4,768]{1,0:T(4,128)(2,1)S(1)} %collective-permute-done.10.refs_2_, bf16[4,768]{1,0:T(4,128)(2,1)S(1)} %collective-permute-done.11.refs_3_), custom_call_target="tpu_custom_call" | custom-call | flops 1000000000 | bytes 1048576 | tf_op jit(solution)/shard_map/pallas_call | solution.py:187
  (12 shorter events, 0.0 us)
Async XLA Ops:
  0.6 4.5 %copy-start.1 = (bf16[1,4,3072]{2,1,0:T(4,128)(2,1)S(1)}, bf16[1,4,3072]{2,1,0:T(4,128)(2,1)}, u32[]{:S(2)}) copy-start(bf16[1,4,3072]{2,1,0:T(4,128)(2,1)} %param.8) | copy-start | bytes 73732
  0.6 4.5 %copy-start.5 = (s32[4]{0:T(128)S(1)}, s32[4]{0:T(128)}, u32[]{:S(2)}) copy-start(s32[4]{0:T(128)} %param.14) | copy-start | bytes 52
  0.6 4.5 %copy-start.4 = (bf16[1,4,4,2,3072]{4,3,2,1,0:T(2,128)(2,1)S(1)}, bf16[1,4,4,2,3072]{4,3,2,1,0:T(2,128)(2,1)}, u32[]{:S(2)}) copy-start(bf16[1,4,4,2,3072]{4,3,2,1,0:T(2,128)(2,1)} %cache_ref.3) | copy-start | bytes 589828
  0.7 8.6 %collective-permute-start.1 = (bf16[4,3072]{1,0:T(4,128)(2,1)}, bf16[4,3072]{1,0:T(4,128)(2,1)S(1)}, u32[]{:S(2)}, u32[]{:S(2)}) collective-permute-start(bf16[4,3072]{1,0:T(4,128)(2,1)} %bitcast.21), channel_id=1, source_target_pairs={{0,8},{4,12},{8,0},{12,4},{1,9},{5,13},{9,1},{13,5},{2,10},{6,14},... | collective-permute-start | bytes 73736 | tf_op jit(solution)/shard_map/ppermute | solution.py:215
  3.9 5.4 %collective-permute-start.2 = (bf16[4,3072]{1,0:T(4,128)(2,1)}, bf16[4,3072]{1,0:T(4,128)(2,1)S(1)}, u32[]{:S(2)}, u32[]{:S(2)}) collective-permute-start(bf16[4,3072]{1,0:T(4,128)(2,1)} %bitcast.22), channel_id=1, source_target_pairs={{0,4},{4,0},{8,12},{12,8},{1,5},{5,1},{9,13},{13,9},{2,6},{6,2},{1... | collective-permute-start | bytes 73736 | tf_op jit(solution)/shard_map/ppermute | solution.py:215
  5.2 5.3 %slice-start = ((s8[14155776]{0:T(1024)(128)(4,1)}), s8[4194304]{0:T(1024)(128)(4,1)S(1)}, s32[]{:S(2)}) async-start(s8[14155776]{0:T(1024)(128)(4,1)} %bitcast.11), calls=%async_computation | async-start | bytes 8388608
  5.2 5.3 %slice-start.1 = ((s8[14155776]{0:T(1024)(128)(4,1)}), s8[4194304]{0:T(1024)(128)(4,1)S(1)}, s32[]{:S(2)}) async-start(s8[14155776]{0:T(1024)(128)(4,1)} %bitcast.11), calls=%async_computation.1 | async-start | bytes 8388608
  5.2 5.3 %copy-start = (f32[1,4,3,3072]{3,1,2,0:T(4,128)S(1)}, f32[1,4,3,3072]{3,1,2,0:T(4,128)}, u32[]{:S(2)}) copy-start(f32[1,4,3,3072]{3,1,2,0:T(4,128)} %param.13) | copy-start | bytes 442372
  5.2 5.2 %copy-start.2 = (f32[1,2,128]{2,1,0:T(2,128)S(1)}, f32[1,2,128]{2,1,0:T(2,128)}, u32[]{:S(2)}) copy-start(f32[1,2,128]{2,1,0:T(2,128)} %param.12) | copy-start | bytes 3076
  5.2 5.2 %copy-start.3 = (s32[4]{0:T(128)S(1)}, s32[4]{0:T(128)}, u32[]{:S(2)}) copy-start(s32[4]{0:T(128)} %param.15) | copy-start | bytes 52
  5.3 5.1 %slice-start.2 = ((s8[14155776]{0:T(1024)(128)(4,1)}), s8[4194304]{0:T(1024)(128)(4,1)S(1)}, s32[]{:S(2)}) async-start(s8[14155776]{0:T(1024)(128)(4,1)} %bitcast.11), calls=%async_computation.2 | async-start | bytes 8388608
  5.4 5.1 %slice-start.3 = ((s8[14155776]{0:T(1024)(128)(4,1)}), s8[1572864]{0:T(1024)(128)(4,1)S(1)}, s32[]{:S(2)}) async-start(s8[14155776]{0:T(1024)(128)(4,1)} %bitcast.11), calls=%async_computation.3 | async-start | bytes 3145728
  5.4 5.1 %collective-permute-start = (bf16[40,768]{1,0:T(8,128)(2,1)S(1)}, bf16[40,768]{1,0:T(8,128)(2,1)S(1)}, u32[]{:S(2)}, u32[]{:S(2)}) collective-permute-start(bf16[40,768]{1,0:T(8,128)(2,1)S(1)} %shard_map.96), channel_id=1, source_target_pairs={{0,12},{4,8},{8,4},{12,0},{1,13},{5,9},{9,5},{13,1},{2,14},{6,10},... | collective-permute-start | bytes 184328 | tf_op jit(solution)/shard_map/ppermute | solution.py:215
  6.2 6.0 %collective-permute-start.3 = (bf16[24,768]{1,0:T(8,128)(2,1)S(1)}, bf16[24,768]{1,0:T(8,128)(2,1)S(1)}, u32[]{:S(2)}, u32[]{:S(2)}) collective-permute-start(bf16[24,768]{1,0:T(8,128)(2,1)S(1)} %get-tuple-element.23), channel_id=1, source_target_pairs={{0,8},{4,12},{8,0},{12,4},{1,9},{5,13},{9,1},{13,5},{2,10},{6,14},... | collective-permute-start | bytes 110600 | tf_op jit(solution)/shard_map/ppermute | solution.py:215
  7.0 5.1 %collective-permute-start.4 = (bf16[24,768]{1,0:T(8,128)(2,1)S(1)}, bf16[24,768]{1,0:T(8,128)(2,1)S(1)}, u32[]{:S(2)}, u32[]{:S(2)}) collective-permute-start(bf16[24,768]{1,0:T(8,128)(2,1)S(1)} %get-tuple-element.24), channel_id=1, source_target_pairs={{0,4},{4,0},{8,12},{12,8},{1,5},{5,1},{9,13},{13,9},{2,6},{6,2},{1... | collective-permute-start | bytes 110600 | tf_op jit(solution)/shard_map/ppermute | solution.py:215
  10.5 6.9 %slice-start.4 = ((s8[4718592]{0:T(1024)(128)(4,1)}), s8[4194304]{0:T(1024)(128)(4,1)S(1)}, s32[]{:S(2)}) async-start(s8[4718592]{0:T(1024)(128)(4,1)} %bitcast.15), calls=%async_computation.4 | async-start | bytes 8388608
  12.2 5.2 %slice-start.5 = ((s8[4718592]{0:T(1024)(128)(4,1)}), s8[524288]{0:T(1024)(128)(4,1)S(1)}, s32[]{:S(2)}) async-start(s8[4718592]{0:T(1024)(128)(4,1)} %bitcast.15), calls=%async_computation.5 | async-start | bytes 1048576
  13.2 4.2 %collective-permute-start.6 = (bf16[24,768]{1,0:T(8,128)(2,1)S(1)}, bf16[24,768]{1,0:T(8,128)(2,1)S(1)}, u32[]{:S(2)}, u32[]{:S(2)}) collective-permute-start(bf16[24,768]{1,0:T(8,128)(2,1)S(1)} %get-tuple-element.28), channel_id=1, source_target_pairs={{0,8},{4,12},{8,0},{12,4},{1,9},{5,13},{9,1},{13,5},{2,10},{6,14},... | collective-permute-start | bytes 110600 | tf_op jit(solution)/shard_map/ppermute | solution.py:215
  13.3 4.7 %collective-permute-start.5 = (bf16[24,768]{1,0:T(8,128)(2,1)S(1)}, bf16[24,768]{1,0:T(8,128)(2,1)S(1)}, u32[]{:S(2)}, u32[]{:S(2)}) collective-permute-start(bf16[24,768]{1,0:T(8,128)(2,1)S(1)} %get-tuple-element.26), channel_id=1, source_target_pairs={{0,12},{4,8},{8,4},{12,0},{1,13},{5,9},{9,5},{13,1},{2,14},{6,10},... | collective-permute-start | bytes 110600 | tf_op jit(solution)/shard_map/ppermute | solution.py:215
  15.7 2.8 %collective-permute-start.7 = (bf16[24,768]{1,0:T(8,128)(2,1)S(1)}, bf16[24,768]{1,0:T(8,128)(2,1)S(1)}, u32[]{:S(2)}, u32[]{:S(2)}) collective-permute-start(bf16[24,768]{1,0:T(8,128)(2,1)S(1)} %get-tuple-element.29), channel_id=1, source_target_pairs={{0,4},{4,0},{8,12},{12,8},{1,5},{5,1},{9,13},{13,9},{2,6},{6,2},{1... | collective-permute-start | bytes 110600 | tf_op jit(solution)/shard_map/ppermute | solution.py:215
  18.8 9.0 %collective-permute-start.8 = (bf16[4,768]{1,0:T(4,128)(2,1)S(1)}, bf16[4,768]{1,0:T(4,128)(2,1)S(1)}, u32[]{:S(2)}, u32[]{:S(2)}) collective-permute-start(bf16[4,768]{1,0:T(4,128)(2,1)S(1)} %get-tuple-element.30), channel_id=1, source_target_pairs={{0,5},{1,2},{2,7},{3,0},{4,1},{5,6},{6,3},{7,4},{8,13},{9,10},{10,... | collective-permute-start | bytes 18440 | tf_op jit(solution)/shard_map/ppermute | solution.py:223
  24.4 4.0 %collective-permute-start.9 = (bf16[4,768]{1,0:T(4,128)(2,1)S(1)}, bf16[4,768]{1,0:T(4,128)(2,1)S(1)}, u32[]{:S(2)}, u32[]{:S(2)}) collective-permute-start(bf16[4,768]{1,0:T(4,128)(2,1)S(1)} %get-tuple-element.31), channel_id=1, source_target_pairs={{0,9},{1,6},{2,11},{3,4},{4,13},{5,2},{6,15},{7,0},{8,1},{9,14},{1... | collective-permute-start | bytes 18440 | tf_op jit(solution)/shard_map/ppermute | solution.py:223
  24.5 4.0 %collective-permute-start.10 = (bf16[4,768]{1,0:T(4,128)(2,1)S(1)}, bf16[4,768]{1,0:T(4,128)(2,1)S(1)}, u32[]{:S(2)}, u32[]{:S(2)}) collective-permute-start(bf16[4,768]{1,0:T(4,128)(2,1)S(1)} %get-tuple-element.32), channel_id=1, source_target_pairs={{0,1},{1,14},{2,3},{3,12},{4,5},{5,10},{6,7},{7,8},{8,9},{9,6},{10... | collective-permute-start | bytes 18440 | tf_op jit(solution)/shard_map/ppermute | solution.py:223
  26.9 4.9 %collective-permute-start.11 = (bf16[4,768]{1,0:T(4,128)(2,1)S(1)}, bf16[4,768]{1,0:T(4,128)(2,1)S(1)}, u32[]{:S(2)}, u32[]{:S(2)}) collective-permute-start(bf16[4,768]{1,0:T(4,128)(2,1)S(1)} %get-tuple-element.33), channel_id=1, source_target_pairs={{0,13},{1,10},{2,15},{3,8},{4,9},{5,14},{6,11},{7,12},{8,5},{9,2},... | collective-permute-start | bytes 18440 | tf_op jit(solution)/shard_map/ppermute | solution.py:223
where the time goes:
time: 32.5 us; the launch traced here: 32.4 us
  starting transfers between devices  19.2 us (59%)
  waiting for transfers between devices  7.03 us (22%)
  Pallas kernels  5.26 us (16%)
  between operations  0.84 us (3%)
    ppermute x8, starting transfers between devices, moved(): return lax.ppermute(array, 'seq', [(j, j ^ number) for j in range(slots)])  10.9 us
    ppermute x4, starting transfers between devices, onward(): return lax.ppermute(array, ('seq', 'section'), pairs)  8.28 us
    pallas_call x10, Pallas kernels, call(): pl.pallas_call(functools.partial(kernel, **sizes), out_shape=out_shape, i...  5.26 us
    ppermute x4, waiting for transfers between devices, onward(): return lax.ppermute(array, ('seq', 'section'), pairs)  3.97 us
    ppermute x8, waiting for transfers between devices, moved(): return lax.ppermute(array, 'seq', [(j, j ^ number) for j in range(slots)])  3.06 us
  transfers between devices with their start and end apart: 12, of which 6 were waited for; matrix products, arithmetic and copies ran while one was open for 0% of the time, Pallas kernels for 10%

commit v1 on v0

--- a/solution.py
+++ b/solution.py
@@ -10,7 +10,12 @@
 
 
 APART = (1, 2)
-TURNS = ((3, 2), (0, 3), (2, 1), (1, 0))
+TURNS = (
+    ((3, 2, 1, 0), (1, 2, 0, 3)),
+    ((0, 1, 2, 3), (2, 3, 1, 0)),
+    ((1, 3, 0, 2), (3, 0, 2, 1)),
+    ((2, 0, 3, 1), (0, 1, 3, 2)),
+)
 
 F32 = jnp.float32
 BF16 = jnp.bfloat16
@@ -148,6 +153,17 @@
     refs[-1][...] = total
 
 
+def peer(turn, section):
+    mine = lax.axis_index("seq")
+    entries = []
+    for targets in turn:
+        found = targets[0]
+        for j in range(1, len(targets)):
+            found = jnp.where(mine == j, targets[j], found)
+        entries.append(found)
+    return jnp.where(lax.rem(section, 2) == 0, entries[0], entries[1])
+
+
 def output_kernel(gate_ref, held_ref, weight_ref, total_ref, attention_ref, *outs, number, tokens, turns):
     columns = weight_ref.shape[1]
     start = pl.multiple_of((lax.axis_index("seq") ^ number) * columns, columns)
@@ -157,18 +173,23 @@
     )
     block = held_ref[...].astype(F32) + gate_ref[...] * total.astype(BF16).astype(F32)
     pieces = [block[b * tokens : (b + 1) * tokens] for b in range(len(outs))]
-    even = lax.rem(lax.axis_index("section"), 2) == 0
-    for out, (b, c) in zip(outs, turns, strict=True):
-        out[...] = jnp.where(even, pieces[b], pieces[c]).astype(BF16)
+    mine = lax.axis_index("seq")
+    for out, turn in zip(outs, turns, strict=True):
+        slot = mine ^ peer(turn, lax.axis_index("section"))
+        piece = pieces[0]
+        for b in range(1, len(pieces)):
+            piece = jnp.where(slot == b, pieces[b], piece)
+        out[...] = piece.astype(BF16)
 
 
 def place_kernel(*refs, slots, turns):
     out_ref, refs = refs[slots], refs[:slots][::-1]
     columns = refs[0].shape[1]
-    mine, sections = lax.axis_index("seq"), lax.axis_size("section")
-    even = lax.rem(lax.axis_index("section") + (sections - 1), sections) % 2 == 0
-    for ref, (b, c) in zip(refs, turns, strict=True):
-        start = pl.multiple_of((mine ^ jnp.where(even, b, c)) * columns, columns)
+    sections = lax.axis_size("section")
+    before = lax.rem(lax.axis_index("section") + (sections - 1), sections)
+    for ref, turn in zip(refs, turns, strict=True):
+        back = [[targets.index(j) for j in range(slots)] for targets in turn]
+        start = pl.multiple_of(peer(back, before) * columns, columns)
         out_ref[0, :, pl.ds(start, columns)] = ref[...]
 
 
@@ -206,7 +227,7 @@
     columns, size = w_qkv.shape[3], norm_gain.shape[2]
     heads, stale, rows = columns // size, (patches - 1) * tokens, slots * tokens
     split = apart(slots)
-    turns = TURNS if slots == 4 else [(b, b) for b in range(slots)]
+    turns = TURNS if slots == 4 else [([j ^ b for j in range(slots)],) * 2 for b in range(slots)]
 
     def array(*shape, dtype=BF16):
         return jax.ShapeDtypeStruct(shape, dtype)
@@ -214,9 +235,10 @@
     def moved(array, number):
         return lax.ppermute(array, "seq", [(j, j ^ number) for j in range(slots)])
 
-    def onward(array, turn):
+    def onward(array, number):
+        turn = turns[number]
         pairs = [
-            (j * sections + s, (j ^ turn[s % 2]) * sections + (s + 1) % sections)
+            (j * sections + s, turn[s % 2][j] * sections + (s + 1) % sections)
             for j in range(slots)
             for s in range(sections)
         ]
@@ -302,7 +324,7 @@
         tokens=tokens,
         turns=turns,
     )
-    arrived = [onward(piece, turn) for piece, turn in zip(pieces, turns, strict=True)]
+    arrived = [onward(piece, number) for number, piece in enumerate(pieces)]
     fresh_kv = call(place_kv_kernel, 1e9, array(1, tokens, 2, width), attention[::-1], slots=slots, tokens=tokens)
     next_hidden = call(place_kernel, 1e9, array(1, tokens, width), arrived[::-1], slots=slots, turns=turns)
     return (next_hidden, fresh_kv)

time: 32.5 us -> 32.7 us (level)
  no operation moved by 1% of the time
where the time goes in v1:
time: 32.7 us; the launch traced here: 32.5 us
  starting transfers between devices  19.2 us (59%)
  waiting for transfers between devices  7.2 us (22%)
  Pallas kernels  5.27 us (16%)
  between operations  0.84 us (3%)
    ppermute x8, starting transfers between devices, moved(): return lax.ppermute(array, 'seq', [(j, j ^ number) for j in range(slots)])  10.9 us
    ppermute x4, starting transfers between devices, onward(): return lax.ppermute(array, ('seq', 'section'), pairs)  8.28 us
    pallas_call x10, Pallas kernels, call(): pl.pallas_call(functools.partial(kernel, **sizes), out_shape=out_shape, i...  5.27 us
    ppermute x4, waiting for transfers between devices, onward(): return lax.ppermute(array, ('seq', 'section'), pairs)  4.14 us
    ppermute x8, waiting for transfers between devices, moved(): return lax.ppermute(array, 'seq', [(j, j ^ number) for j in range(slots)])  3.06 us
  transfers between devices with their start and end apart: 12, of which 6 were waited for; matrix products, arithmetic and copies ran while one was open for 0% of the time, Pallas kernels for 10%

profile of v1, /device:TPU:1, one launch (start us, length us, event | category | flops | bytes accessed | tf_op | source)
XLA Modules:
  0.0 32.5 jit_solution(3720528721110615794)
XLA Ops:
  0.6 0.0 copy-start.1
  0.6 0.0 copy-start.5
  0.6 0.0 copy-start.4
  0.7 3.2 %collective-permute-start.1 = (bf16[4,3072]{1,0:T(4,128)(2,1)}, bf16[4,3072]{1,0:T(4,128)(2,1)S(1)}, u32[]{:S(2)}, u32[]{:S(2)}) collective-permute-start(bf16[4,3072]{1,0:T(4,128)(2,1)} %bitcast.21), channel_id=1, source_target_pairs={{0,8},{4,12},{8,0},{12,4},{1,9},{5,13},{9,1},{13,5},{2,10},{6,14},... | collective-permute-start | bytes 73736 | tf_op jit(solution)/shard_map/ppermute | solution.py:236
  3.9 1.3 %collective-permute-start.2 = (bf16[4,3072]{1,0:T(4,128)(2,1)}, bf16[4,3072]{1,0:T(4,128)(2,1)S(1)}, u32[]{:S(2)}, u32[]{:S(2)}) collective-permute-start(bf16[4,3072]{1,0:T(4,128)(2,1)} %bitcast.22), channel_id=1, source_target_pairs={{0,4},{4,0},{8,12},{12,8},{1,5},{5,1},{9,13},{13,9},{2,6},{6,2},{1... | collective-permute-start | bytes 73736 | tf_op jit(solution)/shard_map/ppermute | solution.py:236
  5.2 0.0 copy-done.4
  5.2 0.0 slice-start
  5.2 0.0 slice-start.1
  5.2 0.0 copy-start
  5.2 0.0 copy-start.2
  5.2 0.0 copy-start.3
  5.2 0.1 shard_map.96
  5.3 0.0 slice-start.2
  5.4 0.0 slice-start.3
  5.4 0.6 %collective-permute-start = (bf16[40,768]{1,0:T(8,128)(2,1)S(1)}, bf16[40,768]{1,0:T(8,128)(2,1)S(1)}, u32[]{:S(2)}, u32[]{:S(2)}) collective-permute-start(bf16[40,768]{1,0:T(8,128)(2,1)S(1)} %shard_map.96), channel_id=1, source_target_pairs={{0,12},{4,8},{8,4},{12,0},{1,13},{5,9},{9,5},{13,1},{2,14},{6,10},... | collective-permute-start | bytes 184328 | tf_op jit(solution)/shard_map/ppermute | solution.py:236
  6.0 0.2 shard_map.98
  6.2 0.9 %collective-permute-start.3 = (bf16[24,768]{1,0:T(8,128)(2,1)S(1)}, bf16[24,768]{1,0:T(8,128)(2,1)S(1)}, u32[]{:S(2)}, u32[]{:S(2)}) collective-permute-start(bf16[24,768]{1,0:T(8,128)(2,1)S(1)} %get-tuple-element.23), channel_id=1, source_target_pairs={{0,8},{4,12},{8,0},{12,4},{1,9},{5,13},{9,1},{13,5},{2,10},{6,14},... | collective-permute-start | bytes 110600 | tf_op jit(solution)/shard_map/ppermute | solution.py:236
  7.0 2.2 %collective-permute-start.4 = (bf16[24,768]{1,0:T(8,128)(2,1)S(1)}, bf16[24,768]{1,0:T(8,128)(2,1)S(1)}, u32[]{:S(2)}, u32[]{:S(2)}) collective-permute-start(bf16[24,768]{1,0:T(8,128)(2,1)S(1)} %get-tuple-element.24), channel_id=1, source_target_pairs={{0,4},{4,0},{8,12},{12,8},{1,5},{5,1},{9,13},{13,9},{2,6},{6,2},{1... | collective-permute-start | bytes 110600 | tf_op jit(solution)/shard_map/ppermute | solution.py:236
  9.2 0.0 collective-permute-done.1.refs_1_
  9.2 0.0 collective-permute-done.2.refs_2_
  9.2 1.2 %collective-permute-done.refs_0_ = bf16[40,768]{1,0:T(8,128)(2,1)S(1)} collective-permute-done((bf16[40,768]{1,0:T(8,128)(2,1)S(1)}, bf16[40,768]{1,0:T(8,128)(2,1)S(1)}, u32[]{:S(2)}, u32[]{:S(2)}) %collective-permute-start) | collective-permute-done | bytes 61472 | tf_op jit(solution)/shard_map/ppermute | solution.py:236
  10.4 0.0 slice-done
  10.4 0.0 copy-done
  10.5 0.0 slice-start.4
  10.5 1.6 %shard_map.97 = (bf16[16,768]{1,0:T(8,128)(2,1)S(1)}, bf16[16,768]{1,0:T(8,128)(2,1)S(1)}, bf16[16,3072]{1,0:T(8,128)(2,1)S(1)}, bf16[16,768]{1,0:T(8,128)(2,1)S(1)}, f32[1,768]{1,0:T(1,128)S(1)}) custom-call(s32[1,4]{1,0:T(1,128)S(1)} %bitcast.27, f32[3,4,3072]{2,1,0:T(4,128)S(1)} %bitcast.20, f32[2,128]{1,0:T(2,128)S(1)} %bitcast.26, ...), custom_call_target="tpu_custom_call" | custom-call | flops 2000000000 | bytes 1048576 | tf_op jit(solution)/shard_map/pallas_call | solution.py:208
  12.2 0.0 collective-permute-done.3.refs_1_
  12.2 0.0 collective-permute-done.4.refs_2_
  12.2 0.0 slice-start.5
  12.2 1.0 %shard_map.99 = (bf16[24,768]{1,0:T(8,128)(2,1)S(1)}, bf16[24,768]{1,0:T(8,128)(2,1)S(1)}, bf16[24,768]{1,0:T(8,128)(2,1)S(1)}, bf16[24,768]{1,0:T(8,128)(2,1)S(1)}) custom-call(bf16[16,768]{1,0:T(8,128)(2,1)S(1)} %get-tuple-element.20.q_ref, bf16[16,768]{1,0:T(8,128)(2,1)S(1)} %get-tuple-element.21.k_ref, ...), custom_call_target="tpu_custom_call" | custom-call | flops 2000000000 | bytes 1048576 | tf_op jit(solution)/shard_map/pallas_call | solution.py:208
  13.2 0.1 collective-permute-start.6
  13.3 2.4 %collective-permute-start.5 = (bf16[24,768]{1,0:T(8,128)(2,1)S(1)}, bf16[24,768]{1,0:T(8,128)(2,1)S(1)}, u32[]{:S(2)}, u32[]{:S(2)}) collective-permute-start(bf16[24,768]{1,0:T(8,128)(2,1)S(1)} %get-tuple-element.26), channel_id=1, source_target_pairs={{0,12},{4,8},{8,4},{12,0},{1,13},{5,9},{9,5},{13,1},{2,14},{6,10},... | collective-permute-start | bytes 110600 | tf_op jit(solution)/shard_map/ppermute | solution.py:236
  15.7 0.2 collective-permute-start.7
  15.9 1.5 %collective-permute-done.6.refs_1_ = bf16[24,768]{1,0:T(8,128)(2,1)S(1)} collective-permute-done((bf16[24,768]{1,0:T(8,128)(2,1)S(1)}, bf16[24,768]{1,0:T(8,128)(2,1)S(1)}, u32[]{:S(2)}, u32[]{:S(2)}) %collective-permute-start.6) | collective-permute-done | bytes 36896 | tf_op jit(solution)/shard_map/ppermute | solution.py:236
  17.4 0.4 %shard_map.100.refs_1_ = f32[16,768]{1,0:T(8,128)S(1)} custom-call(bf16[3072,768]{1,0:T(8,128)(2,1)S(1)} %bitcast.17, bf16[24,768]{1,0:T(8,128)(2,1)S(1)} %get-tuple-element.27.refs_0_.refs_3_, bf16[24,768]{1,0:T(8,128)(2,1)S(1)} %collective-permute-done.6.refs_1_), custom_call_target="tpu_custom_call" | custom-call | flops 1000000000 | bytes 1048576 | tf_op jit(solution)/shard_map/pallas_call | solution.py:208
  17.8 0.2 collective-permute-done.5.refs_0_
  18.0 0.3 shard_map.101.total_ref
  18.2 0.3 collective-permute-done.7.attention_ref.refs_2_
  18.5 0.3 shard_map.102
  18.8 5.7 %collective-permute-start.8 = (bf16[4,768]{1,0:T(4,128)(2,1)S(1)}, bf16[4,768]{1,0:T(4,128)(2,1)S(1)}, u32[]{:S(2)}, u32[]{:S(2)}) collective-permute-start(bf16[4,768]{1,0:T(4,128)(2,1)S(1)} %get-tuple-element.30), channel_id=1, source_target_pairs={{0,9},{1,2},{2,11},{3,0},{4,1},{5,6},{6,3},{7,4},{8,13},{9,14},{10... | collective-permute-start | bytes 18440 | tf_op jit(solution)/shard_map/ppermute | solution.py:245
  24.5 1.6 %collective-permute-start.9 = (bf16[4,768]{1,0:T(4,128)(2,1)S(1)}, bf16[4,768]{1,0:T(4,128)(2,1)S(1)}, u32[]{:S(2)}, u32[]{:S(2)}) collective-permute-start(bf16[4,768]{1,0:T(4,128)(2,1)S(1)} %get-tuple-element.31), channel_id=1, source_target_pairs={{0,5},{1,14},{2,7},{3,12},{4,13},{5,2},{6,15},{7,0},{8,1},{9,10},{... | collective-permute-start | bytes 18440 | tf_op jit(solution)/shard_map/ppermute | solution.py:245
  26.0 1.0 %collective-permute-start.10 = (bf16[4,768]{1,0:T(4,128)(2,1)S(1)}, bf16[4,768]{1,0:T(4,128)(2,1)S(1)}, u32[]{:S(2)}, u32[]{:S(2)}) collective-permute-start(bf16[4,768]{1,0:T(4,128)(2,1)S(1)} %get-tuple-element.32), channel_id=1, source_target_pairs={{0,1},{1,10},{2,3},{3,8},{4,5},{5,14},{6,7},{7,12},{8,9},{9,6},{10... | collective-permute-start | bytes 18440 | tf_op jit(solution)/shard_map/ppermute | solution.py:245
  27.1 0.0 collective-permute-start.11
  27.1 0.7 %shard_map.104 = bf16[1,4,2,3072]{3,2,1,0:T(2,128)(2,1)} custom-call(bf16[24,768]{1,0:T(8,128)(2,1)S(1)} %collective-permute-done.5.refs_0_, bf16[24,768]{1,0:T(8,128)(2,1)S(1)} %collective-permute-done.6.refs_1_, bf16[24,768]{1,0:T(8,128)(2,1)S(1)} %collective-permute-done.7.attention_ref.refs_2_, bf16[24,768]{1,0:T(8,128)(2,1)S(1)} %get-tuple-element.27.refs_0_.refs_3_), custom_call_target="tpu_custom_call" | custom-call | flops 1000000000 | bytes 1048576 | tf_op jit(solution)/shard_map/pallas_call | solution.py:208
  27.8 0.0 collective-permute-done.8.refs_0_
  27.8 0.6 %collective-permute-done.9.refs_1_ = bf16[4,768]{1,0:T(4,128)(2,1)S(1)} collective-permute-done((bf16[4,768]{1,0:T(4,128)(2,1)S(1)}, bf16[4,768]{1,0:T(4,128)(2,1)S(1)}, u32[]{:S(2)}, u32[]{:S(2)}) %collective-permute-start.9) | collective-permute-done | bytes 6176 | tf_op jit(solution)/shard_map/ppermute | solution.py:245
  28.4 0.0 collective-permute-done.10.refs_2_
  28.4 3.5 %collective-permute-done.11.refs_3_ = bf16[4,768]{1,0:T(4,128)(2,1)S(1)} collective-permute-done((bf16[4,768]{1,0:T(4,128)(2,1)S(1)}, bf16[4,768]{1,0:T(4,128)(2,1)S(1)}, u32[]{:S(2)}, u32[]{:S(2)}) %collective-permute-start.11) | collective-permute-done | bytes 6176 | tf_op jit(solution)/shard_map/ppermute | solution.py:245
  31.9 0.6 %shard_map.103 = bf16[1,4,3072]{2,1,0:T(4,128)(2,1)} custom-call(bf16[4,768]{1,0:T(4,128)(2,1)S(1)} %collective-permute-done.8.refs_0_, bf16[4,768]{1,0:T(4,128)(2,1)S(1)} %collective-permute-done.9.refs_1_, bf16[4,768]{1,0:T(4,128)(2,1)S(1)} %collective-permute-done.10.refs_2_, bf16[4,768]{1,0:T(4,128)(2,1)S(1)} %collective-permute-done.11.refs_3_), custom_call_target="tpu_custom_call" | custom-call | flops 1000000000 | bytes 1048576 | tf_op jit(solution)/shard_map/pallas_call | solution.py:208
  (12 shorter events, 0.0 us)
Async XLA Ops:
  0.6 4.5 %copy-start.1 = (bf16[1,4,3072]{2,1,0:T(4,128)(2,1)S(1)}, bf16[1,4,3072]{2,1,0:T(4,128)(2,1)}, u32[]{:S(2)}) copy-start(bf16[1,4,3072]{2,1,0:T(4,128)(2,1)} %param.8) | copy-start | bytes 73732
  0.6 4.5 %copy-start.5 = (s32[4]{0:T(128)S(1)}, s32[4]{0:T(128)}, u32[]{:S(2)}) copy-start(s32[4]{0:T(128)} %param.14) | copy-start | bytes 52
  0.6 4.5 %copy-start.4 = (bf16[1,4,4,2,3072]{4,3,2,1,0:T(2,128)(2,1)S(1)}, bf16[1,4,4,2,3072]{4,3,2,1,0:T(2,128)(2,1)}, u32[]{:S(2)}) copy-start(bf16[1,4,4,2,3072]{4,3,2,1,0:T(2,128)(2,1)} %cache_ref.3) | copy-start | bytes 589828
  0.7 8.6 %collective-permute-start.1 = (bf16[4,3072]{1,0:T(4,128)(2,1)}, bf16[4,3072]{1,0:T(4,128)(2,1)S(1)}, u32[]{:S(2)}, u32[]{:S(2)}) collective-permute-start(bf16[4,3072]{1,0:T(4,128)(2,1)} %bitcast.21), channel_id=1, source_target_pairs={{0,8},{4,12},{8,0},{12,4},{1,9},{5,13},{9,1},{13,5},{2,10},{6,14},... | collective-permute-start | bytes 73736 | tf_op jit(solution)/shard_map/ppermute | solution.py:236
  3.9 5.4 %collective-permute-start.2 = (bf16[4,3072]{1,0:T(4,128)(2,1)}, bf16[4,3072]{1,0:T(4,128)(2,1)S(1)}, u32[]{:S(2)}, u32[]{:S(2)}) collective-permute-start(bf16[4,3072]{1,0:T(4,128)(2,1)} %bitcast.22), channel_id=1, source_target_pairs={{0,4},{4,0},{8,12},{12,8},{1,5},{5,1},{9,13},{13,9},{2,6},{6,2},{1... | collective-permute-start | bytes 73736 | tf_op jit(solution)/shard_map/ppermute | solution.py:236
  5.2 5.3 %slice-start = ((s8[14155776]{0:T(1024)(128)(4,1)}), s8[4194304]{0:T(1024)(128)(4,1)S(1)}, s32[]{:S(2)}) async-start(s8[14155776]{0:T(1024)(128)(4,1)} %bitcast.11), calls=%async_computation | async-start | bytes 8388608
  5.2 5.3 %slice-start.1 = ((s8[14155776]{0:T(1024)(128)(4,1)}), s8[4194304]{0:T(1024)(128)(4,1)S(1)}, s32[]{:S(2)}) async-start(s8[14155776]{0:T(1024)(128)(4,1)} %bitcast.11), calls=%async_computation.1 | async-start | bytes 8388608
  5.2 5.3 %copy-start = (f32[1,4,3,3072]{3,1,2,0:T(4,128)S(1)}, f32[1,4,3,3072]{3,1,2,0:T(4,128)}, u32[]{:S(2)}) copy-start(f32[1,4,3,3072]{3,1,2,0:T(4,128)} %param.13) | copy-start | bytes 442372
  5.2 5.2 %copy-start.2 = (f32[1,2,128]{2,1,0:T(2,128)S(1)}, f32[1,2,128]{2,1,0:T(2,128)}, u32[]{:S(2)}) copy-start(f32[1,2,128]{2,1,0:T(2,128)} %param.12) | copy-start | bytes 3076
  5.2 5.2 %copy-start.3 = (s32[4]{0:T(128)S(1)}, s32[4]{0:T(128)}, u32[]{:S(2)}) copy-start(s32[4]{0:T(128)} %param.15) | copy-start | bytes 52
  5.3 5.1 %slice-start.2 = ((s8[14155776]{0:T(1024)(128)(4,1)}), s8[4194304]{0:T(1024)(128)(4,1)S(1)}, s32[]{:S(2)}) async-start(s8[14155776]{0:T(1024)(128)(4,1)} %bitcast.11), calls=%async_computation.2 | async-start | bytes 8388608
  5.4 5.1 %slice-start.3 = ((s8[14155776]{0:T(1024)(128)(4,1)}), s8[1572864]{0:T(1024)(128)(4,1)S(1)}, s32[]{:S(2)}) async-start(s8[14155776]{0:T(1024)(128)(4,1)} %bitcast.11), calls=%async_computation.3 | async-start | bytes 3145728
  5.4 5.1 %collective-permute-start = (bf16[40,768]{1,0:T(8,128)(2,1)S(1)}, bf16[40,768]{1,0:T(8,128)(2,1)S(1)}, u32[]{:S(2)}, u32[]{:S(2)}) collective-permute-start(bf16[40,768]{1,0:T(8,128)(2,1)S(1)} %shard_map.96), channel_id=1, source_target_pairs={{0,12},{4,8},{8,4},{12,0},{1,13},{5,9},{9,5},{13,1},{2,14},{6,10},... | collective-permute-start | bytes 184328 | tf_op jit(solution)/shard_map/ppermute | solution.py:236
  6.2 6.0 %collective-permute-start.3 = (bf16[24,768]{1,0:T(8,128)(2,1)S(1)}, bf16[24,768]{1,0:T(8,128)(2,1)S(1)}, u32[]{:S(2)}, u32[]{:S(2)}) collective-permute-start(bf16[24,768]{1,0:T(8,128)(2,1)S(1)} %get-tuple-element.23), channel_id=1, source_target_pairs={{0,8},{4,12},{8,0},{12,4},{1,9},{5,13},{9,1},{13,5},{2,10},{6,14},... | collective-permute-start | bytes 110600 | tf_op jit(solution)/shard_map/ppermute | solution.py:236
  7.0 5.1 %collective-permute-start.4 = (bf16[24,768]{1,0:T(8,128)(2,1)S(1)}, bf16[24,768]{1,0:T(8,128)(2,1)S(1)}, u32[]{:S(2)}, u32[]{:S(2)}) collective-permute-start(bf16[24,768]{1,0:T(8,128)(2,1)S(1)} %get-tuple-element.24), channel_id=1, source_target_pairs={{0,4},{4,0},{8,12},{12,8},{1,5},{5,1},{9,13},{13,9},{2,6},{6,2},{1... | collective-permute-start | bytes 110600 | tf_op jit(solution)/shard_map/ppermute | solution.py:236
  10.5 6.9 %slice-start.4 = ((s8[4718592]{0:T(1024)(128)(4,1)}), s8[4194304]{0:T(1024)(128)(4,1)S(1)}, s32[]{:S(2)}) async-start(s8[4718592]{0:T(1024)(128)(4,1)} %bitcast.15), calls=%async_computation.4 | async-start | bytes 8388608
  12.2 5.2 %slice-start.5 = ((s8[4718592]{0:T(1024)(128)(4,1)}), s8[524288]{0:T(1024)(128)(4,1)S(1)}, s32[]{:S(2)}) async-start(s8[4718592]{0:T(1024)(128)(4,1)} %bitcast.15), calls=%async_computation.5 | async-start | bytes 1048576
  13.2 4.2 %collective-permute-start.6 = (bf16[24,768]{1,0:T(8,128)(2,1)S(1)}, bf16[24,768]{1,0:T(8,128)(2,1)S(1)}, u32[]{:S(2)}, u32[]{:S(2)}) collective-permute-start(bf16[24,768]{1,0:T(8,128)(2,1)S(1)} %get-tuple-element.28), channel_id=1, source_target_pairs={{0,8},{4,12},{8,0},{12,4},{1,9},{5,13},{9,1},{13,5},{2,10},{6,14},... | collective-permute-start | bytes 110600 | tf_op jit(solution)/shard_map/ppermute | solution.py:236
  13.3 4.7 %collective-permute-start.5 = (bf16[24,768]{1,0:T(8,128)(2,1)S(1)}, bf16[24,768]{1,0:T(8,128)(2,1)S(1)}, u32[]{:S(2)}, u32[]{:S(2)}) collective-permute-start(bf16[24,768]{1,0:T(8,128)(2,1)S(1)} %get-tuple-element.26), channel_id=1, source_target_pairs={{0,12},{4,8},{8,4},{12,0},{1,13},{5,9},{9,5},{13,1},{2,14},{6,10},... | collective-permute-start | bytes 110600 | tf_op jit(solution)/shard_map/ppermute | solution.py:236
  15.7 2.8 %collective-permute-start.7 = (bf16[24,768]{1,0:T(8,128)(2,1)S(1)}, bf16[24,768]{1,0:T(8,128)(2,1)S(1)}, u32[]{:S(2)}, u32[]{:S(2)}) collective-permute-start(bf16[24,768]{1,0:T(8,128)(2,1)S(1)} %get-tuple-element.29), channel_id=1, source_target_pairs={{0,4},{4,0},{8,12},{12,8},{1,5},{5,1},{9,13},{13,9},{2,6},{6,2},{1... | collective-permute-start | bytes 110600 | tf_op jit(solution)/shard_map/ppermute | solution.py:236
  18.8 9.0 %collective-permute-start.8 = (bf16[4,768]{1,0:T(4,128)(2,1)S(1)}, bf16[4,768]{1,0:T(4,128)(2,1)S(1)}, u32[]{:S(2)}, u32[]{:S(2)}) collective-permute-start(bf16[4,768]{1,0:T(4,128)(2,1)S(1)} %get-tuple-element.30), channel_id=1, source_target_pairs={{0,9},{1,2},{2,11},{3,0},{4,1},{5,6},{6,3},{7,4},{8,13},{9,14},{10... | collective-permute-start | bytes 18440 | tf_op jit(solution)/shard_map/ppermute | solution.py:245
  24.5 4.0 %collective-permute-start.9 = (bf16[4,768]{1,0:T(4,128)(2,1)S(1)}, bf16[4,768]{1,0:T(4,128)(2,1)S(1)}, u32[]{:S(2)}, u32[]{:S(2)}) collective-permute-start(bf16[4,768]{1,0:T(4,128)(2,1)S(1)} %get-tuple-element.31), channel_id=1, source_target_pairs={{0,5},{1,14},{2,7},{3,12},{4,13},{5,2},{6,15},{7,0},{8,1},{9,10},{... | collective-permute-start | bytes 18440 | tf_op jit(solution)/shard_map/ppermute | solution.py:245
  26.0 2.4 %collective-permute-start.10 = (bf16[4,768]{1,0:T(4,128)(2,1)S(1)}, bf16[4,768]{1,0:T(4,128)(2,1)S(1)}, u32[]{:S(2)}, u32[]{:S(2)}) collective-permute-start(bf16[4,768]{1,0:T(4,128)(2,1)S(1)} %get-tuple-element.32), channel_id=1, source_target_pairs={{0,1},{1,10},{2,3},{3,8},{4,5},{5,14},{6,7},{7,12},{8,9},{9,6},{10... | collective-permute-start | bytes 18440 | tf_op jit(solution)/shard_map/ppermute | solution.py:245
  27.1 4.9 %collective-permute-start.11 = (bf16[4,768]{1,0:T(4,128)(2,1)S(1)}, bf16[4,768]{1,0:T(4,128)(2,1)S(1)}, u32[]{:S(2)}, u32[]{:S(2)}) collective-permute-start(bf16[4,768]{1,0:T(4,128)(2,1)S(1)} %get-tuple-element.33), channel_id=1, source_target_pairs={{0,13},{1,6},{2,15},{3,4},{4,9},{5,10},{6,11},{7,8},{8,5},{9,2},{1... | collective-permute-start | bytes 18440 | tf_op jit(solution)/shard_map/ppermute | solution.py:245

commit v2 on v1

--- a/solution.py
+++ b/solution.py
@@ -73,7 +73,7 @@
 
 def project_kernel(step_ref, mod_ref, gain_ref, weight_ref, *refs, slots, tokens, heads, size, stale):
     hidden_refs = refs[:slots][::-1]
-    q_ref, k_ref, normed_ref, held_ref, gate_ref, scratch = refs[slots:]
+    q_ref, k_ref, v_ref, held_ref, gate_ref, scratch = refs[slots:]
     mine = lax.axis_index("seq")
     columns, length = heads * size, slots * tokens
     step = lax.broadcasted_iota(jnp.int32, (mod_ref.shape[1], 1), 0).astype(F32) == entry(step_ref)
@@ -88,20 +88,20 @@
             rows.append(jnp.concatenate([cut[c * tokens : (c + 1) * tokens] for c in range(slots)], axis=1))
     rows = jnp.concatenate(rows, axis=0)
     normed = (layer_norm(rows) * (1.0 + modulate[1]) + modulate[0]).astype(BF16)
-    normed_ref[...] = normed
     for part, out in enumerate((q_ref, k_ref)):
         dotted = jnp.dot(normed, weight_ref[part], preferred_element_type=F32).astype(BF16).astype(F32)
         stacked = jnp.concatenate([dotted[:, h * size : (h + 1) * size] for h in range(heads)], axis=0)
         stacked = head_norm(stacked, gain_ref[pl.ds(part, 1), :]).astype(BF16)
         for h in range(heads):
             out[:, h * size : (h + 1) * size] = stacked[h * length : (h + 1) * length]
+    v_ref[...] = jnp.dot(normed, weight_ref[2], preferred_element_type=F32).astype(BF16)
     scratch[...] = rows
     held_ref[...] = scratch[:, pl.ds(start, columns)].astype(BF16)
     gates = jnp.where(step, mod_ref[2, :, pl.ds(start, columns)], 0.0)
     gate_ref[...] = jnp.sum(gates, axis=0, keepdims=True)
 
 
-def attend_kernel(q_ref, k_ref, normed_ref, weight_ref, *refs, slots, tokens, stale, heads, size):
+def attend_kernel(q_ref, k_ref, v_ref, *refs, slots, tokens, stale, heads, size):
     old, outs = refs[:slots][::-1], refs[slots:]
     old = [r[: 2 * stale].astype(F32) for r in old]
     fresh_keys = k_ref[...].astype(F32)
@@ -114,7 +114,7 @@
     cuts = [slice(h * size, (h + 1) * size) for h in range(heads)]
     dims = (((1,), (1,)), ((), ()))
     scores = [lax.dot_general(queries[:, cut], keys[:, cut], dims, preferred_element_type=F32) for cut in cuts]
-    fresh_values = jnp.dot(normed_ref[...], weight_ref[2], preferred_element_type=F32).astype(BF16).astype(F32)
+    fresh_values = v_ref[...].astype(F32)
     scores = jnp.concatenate(scores, axis=0) / math.sqrt(size)
     top = jnp.max(scores, axis=-1, keepdims=True)
     weights = jnp.exp(scores - top).astype(BF16).astype(F32)
@@ -183,14 +183,19 @@
 
 
 def place_kernel(*refs, slots, turns):
-    out_ref, refs = refs[slots], refs[:slots][::-1]
+    out_ref, sems, refs = refs[slots], refs[slots + 1], refs[:slots][::-1]
     columns = refs[0].shape[1]
     sections = lax.axis_size("section")
     before = lax.rem(lax.axis_index("section") + (sections - 1), sections)
-    for ref, turn in zip(refs, turns, strict=True):
+    copies = []
+    for k, (ref, turn) in enumerate(zip(refs, turns, strict=True)):
         back = [[targets.index(j) for j in range(slots)] for targets in turn]
         start = pl.multiple_of(peer(back, before) * columns, columns)
-        out_ref[0, :, pl.ds(start, columns)] = ref[...]
+        copies.append(pltpu.make_async_copy(ref, out_ref.at[0, :, pl.ds(start, columns)], sems.at[k]))
+    for copy in copies:
+        copy.start()
+    for copy in copies:
+        copy.wait()
 
 
 def place_kv_kernel(*refs, slots, tokens):
@@ -204,12 +209,12 @@
         out_ref[0, :, :, pl.ds(start, columns)] = both.astype(BF16)
 
 
-def call(kernel, flops, out_shape, operands, scratch=(), **sizes):
+def call(kernel, flops, out_shape, operands, scratch=(), out_space=pltpu.VMEM, **sizes):
     return pl.pallas_call(
         functools.partial(kernel, **sizes),
         out_shape=out_shape,
         in_specs=[VMEM] * len(operands),
-        out_specs=jax.tree.map(lambda _: VMEM, out_shape),
+        out_specs=jax.tree.map(lambda _: pl.BlockSpec(memory_space=out_space), out_shape),
         scratch_shapes=scratch,
         compiler_params=pltpu.CompilerParams(vmem_limit_bytes=16 * 2**20),
         cost_estimate=pl.CostEstimate(flops=int(flops), transcendentals=0, bytes_accessed=2**20),
@@ -269,13 +274,13 @@
     old = exchanged(packed)
     inputs = [own] + [alone[b] if b in split else old[b] for b in range(1, slots)]
     weights = jnp.transpose(w_qkv[0], (1, 0, 2))
-    queries, keys, normed, held, gate = call(
+    queries, keys, values, held, gate = call(
         project_kernel,
         2e9,
         [
             array(rows, columns),
             array(rows, columns),
-            array(rows, width),
+            array(rows, columns),
             array(rows, columns),
             array(1, columns, dtype=F32),
         ],
@@ -291,7 +296,7 @@
         attend_kernel,
         2e9,
         [array(rows + 2 * tokens, columns)] * slots,
-        [queries, keys, normed, weights, *old[::-1]],
+        [queries, keys, values, *old[::-1]],
         slots=slots,
         tokens=tokens,
         stale=stale,
@@ -300,7 +305,7 @@
     )
     attention = exchanged(ordered)
     out_weights = w_out[0]
-    groups = [(0, 2), (3,)]
+    groups = [(0, 2), (3,)] if slots == 4 else [(0,)] + [(b,) for b in range(slots - 1, 1, -1)]
     total = []
     for numbers in groups:
         operands = [out_weights] + [attention[b] for b in numbers] + total
@@ -326,7 +331,16 @@
     )
     arrived = [onward(piece, number) for number, piece in enumerate(pieces)]
     fresh_kv = call(place_kv_kernel, 1e9, array(1, tokens, 2, width), attention[::-1], slots=slots, tokens=tokens)
-    next_hidden = call(place_kernel, 1e9, array(1, tokens, width), arrived[::-1], slots=slots, turns=turns)
+    next_hidden = call(
+        place_kernel,
+        1e9,
+        array(1, tokens, width),
+        arrived[::-1],
+        scratch=[pltpu.SemaphoreType.DMA((slots,))],
+        out_space=pl.ANY,
+        slots=slots,
+        turns=turns,
+    )
     return (next_hidden, fresh_kv)
 
 

time: 32.7 us -> 32.6 us (level)
  transfers between devices with their start and end apart: 12 -> 12, of which waited for: 6 -> 6; matrix products, arithmetic and copies ran while one was open for 0% -> 0% of each run, Pallas kernels for 10% -> 12%
where the time goes in v2:
time: 32.6 us; the launch traced here: 32.5 us
  starting transfers between devices  19.3 us (59%)
  waiting for transfers between devices  7.05 us (22%)
  Pallas kernels  5.21 us (16%)
  between operations  0.82 us (3%)
    ppermute x8, starting transfers between devices, moved(): return lax.ppermute(array, 'seq', [(j, j ^ number) for j in range(slots)])  10.9 us
    ppermute x4, starting transfers between devices, onward(): return lax.ppermute(array, ('seq', 'section'), pairs)  8.43 us
    pallas_call x10, Pallas kernels, call(): pl.pallas_call(functools.partial(kernel, **sizes), out_shape=out_shape, i...  5.21 us
    ppermute x4, waiting for transfers between devices, onward(): return lax.ppermute(array, ('seq', 'section'), pairs)  4.14 us
    ppermute x8, waiting for transfers between devices, moved(): return lax.ppermute(array, 'seq', [(j, j ^ number) for j in range(slots)])  2.91 us
  transfers between devices with their start and end apart: 12, of which 6 were waited for; matrix products, arithmetic and copies ran while one was open for 0% of the time, Pallas kernels for 12%

profile of v2, /device:TPU:1, one launch (start us, length us, event | category | flops | bytes accessed | tf_op | source)
XLA Modules:
  0.0 32.5 jit_solution(10497886916278200163)
XLA Ops:
  0.6 0.0 copy-start.1
  0.6 0.0 copy-start.4
  0.6 0.0 copy-start.5
  0.7 2.2 %collective-permute-start.2 = (bf16[4,3072]{1,0:T(4,128)(2,1)}, bf16[4,3072]{1,0:T(4,128)(2,1)S(1)}, u32[]{:S(2)}, u32[]{:S(2)}) collective-permute-start(bf16[4,3072]{1,0:T(4,128)(2,1)} %bitcast.20), channel_id=1, source_target_pairs={{0,4},{4,0},{8,12},{12,8},{1,5},{5,1},{9,13},{13,9},{2,6},{6,2},{1... | collective-permute-start | bytes 73736 | tf_op jit(solution)/shard_map/ppermute | solution.py:241
  2.8 2.3 %collective-permute-start.1 = (bf16[4,3072]{1,0:T(4,128)(2,1)}, bf16[4,3072]{1,0:T(4,128)(2,1)S(1)}, u32[]{:S(2)}, u32[]{:S(2)}) collective-permute-start(bf16[4,3072]{1,0:T(4,128)(2,1)} %bitcast.21), channel_id=1, source_target_pairs={{0,8},{4,12},{8,0},{12,4},{1,9},{5,13},{9,1},{13,5},{2,10},{6,14},... | collective-permute-start | bytes 73736 | tf_op jit(solution)/shard_map/ppermute | solution.py:241
  5.2 0.0 copy-done.5
  5.2 0.0 slice-start.2
  5.2 0.0 slice-start.3
  5.2 0.0 copy-start
  5.2 0.0 copy-start.2
  5.2 0.0 copy-start.3
  5.2 0.1 shard_map.96
  5.3 0.0 slice-start.4
  5.4 0.0 slice-start.5
  5.4 0.6 %collective-permute-start = (bf16[40,768]{1,0:T(8,128)(2,1)S(1)}, bf16[40,768]{1,0:T(8,128)(2,1)S(1)}, u32[]{:S(2)}, u32[]{:S(2)}) collective-permute-start(bf16[40,768]{1,0:T(8,128)(2,1)S(1)} %shard_map.96), channel_id=1, source_target_pairs={{0,12},{4,8},{8,4},{12,0},{1,13},{5,9},{9,5},{13,1},{2,14},{6,10},... | collective-permute-start | bytes 184328 | tf_op jit(solution)/shard_map/ppermute | solution.py:241
  6.0 0.2 shard_map.98
  6.2 0.0 slice-start
  6.2 0.9 %collective-permute-start.3 = (bf16[24,768]{1,0:T(8,128)(2,1)S(1)}, bf16[24,768]{1,0:T(8,128)(2,1)S(1)}, u32[]{:S(2)}, u32[]{:S(2)}) collective-permute-start(bf16[24,768]{1,0:T(8,128)(2,1)S(1)} %get-tuple-element.23), channel_id=1, source_target_pairs={{0,8},{4,12},{8,0},{12,4},{1,9},{5,13},{9,1},{13,5},{2,10},{6,14},... | collective-permute-start | bytes 110600 | tf_op jit(solution)/shard_map/ppermute | solution.py:241
  7.1 2.2 %collective-permute-start.4 = (bf16[24,768]{1,0:T(8,128)(2,1)S(1)}, bf16[24,768]{1,0:T(8,128)(2,1)S(1)}, u32[]{:S(2)}, u32[]{:S(2)}) collective-permute-start(bf16[24,768]{1,0:T(8,128)(2,1)S(1)} %get-tuple-element.24), channel_id=1, source_target_pairs={{0,4},{4,0},{8,12},{12,8},{1,5},{5,1},{9,13},{13,9},{2,6},{6,2},{1... | collective-permute-start | bytes 110600 | tf_op jit(solution)/shard_map/ppermute | solution.py:241
  9.3 0.0 collective-permute-done.2.refs_2_
  9.3 0.0 collective-permute-done.1.refs_1_
  9.3 1.2 %collective-permute-done.refs_0_ = bf16[40,768]{1,0:T(8,128)(2,1)S(1)} collective-permute-done((bf16[40,768]{1,0:T(8,128)(2,1)S(1)}, bf16[40,768]{1,0:T(8,128)(2,1)S(1)}, u32[]{:S(2)}, u32[]{:S(2)}) %collective-permute-start) | collective-permute-done | bytes 61472 | tf_op jit(solution)/shard_map/ppermute | solution.py:241
  10.4 0.0 copy-done
  10.4 0.0 copy-done.2
  10.5 0.0 slice-start.1
  10.5 2.1 %shard_map.97 = (bf16[16,768]{1,0:T(8,128)(2,1)S(1)}, bf16[16,768]{1,0:T(8,128)(2,1)S(1)}, bf16[16,768]{1,0:T(8,128)(2,1)S(1)}, bf16[16,768]{1,0:T(8,128)(2,1)S(1)}, f32[1,768]{1,0:T(1,128)S(1)}) custom-call(s32[1,4]{1,0:T(1,128)S(1)} %bitcast.26, f32[3,4,3072]{2,1,0:T(4,128)S(1)} %bitcast.19, f32[2,128]{1,0:T(2,128)S(1)} %bitcast.25, ...), custom_call_target="tpu_custom_call" | custom-call | flops 2000000000 | bytes 1048576 | tf_op jit(solution)/shard_map/pallas_call | solution.py:213
  12.6 0.0 collective-permute-done.3.refs_1_
  12.6 0.0 collective-permute-done.4.refs_2_
  12.7 0.4 %shard_map.99 = (bf16[24,768]{1,0:T(8,128)(2,1)S(1)}, bf16[24,768]{1,0:T(8,128)(2,1)S(1)}, bf16[24,768]{1,0:T(8,128)(2,1)S(1)}, bf16[24,768]{1,0:T(8,128)(2,1)S(1)}) custom-call(bf16[16,768]{1,0:T(8,128)(2,1)S(1)} %get-tuple-element.20.q_ref, bf16[16,768]{1,0:T(8,128)(2,1)S(1)} %get-tuple-element.21.k_ref, bf16[16,768]{1,0:T(8,128)(2,1)S(1)} %get-tuple-element.22.v_ref, ...), custom_call_target="tpu_custom_call" | custom-call | flops 2000000000 | bytes 1048576 | tf_op jit(solution)/shard_map/pallas_call | solution.py:213
  13.1 0.1 collective-permute-start.6
  13.2 2.1 %collective-permute-start.5 = (bf16[24,768]{1,0:T(8,128)(2,1)S(1)}, bf16[24,768]{1,0:T(8,128)(2,1)S(1)}, u32[]{:S(2)}, u32[]{:S(2)}) collective-permute-start(bf16[24,768]{1,0:T(8,128)(2,1)S(1)} %get-tuple-element.26), channel_id=1, source_target_pairs={{0,12},{4,8},{8,4},{12,0},{1,13},{5,9},{9,5},{13,1},{2,14},{6,10},... | collective-permute-start | bytes 110600 | tf_op jit(solution)/shard_map/ppermute | solution.py:241
  15.3 0.5 %collective-permute-start.7 = (bf16[24,768]{1,0:T(8,128)(2,1)S(1)}, bf16[24,768]{1,0:T(8,128)(2,1)S(1)}, u32[]{:S(2)}, u32[]{:S(2)}) collective-permute-start(bf16[24,768]{1,0:T(8,128)(2,1)S(1)} %get-tuple-element.29), channel_id=1, source_target_pairs={{0,4},{4,0},{8,12},{12,8},{1,5},{5,1},{9,13},{13,9},{2,6},{6,2},{1... | collective-permute-start | bytes 110600 | tf_op jit(solution)/shard_map/ppermute | solution.py:241
  15.8 1.2 %collective-permute-done.6.refs_1_ = bf16[24,768]{1,0:T(8,128)(2,1)S(1)} collective-permute-done((bf16[24,768]{1,0:T(8,128)(2,1)S(1)}, bf16[24,768]{1,0:T(8,128)(2,1)S(1)}, u32[]{:S(2)}, u32[]{:S(2)}) %collective-permute-start.6) | collective-permute-done | bytes 36896 | tf_op jit(solution)/shard_map/ppermute | solution.py:241
  17.0 0.4 %shard_map.100.refs_1_ = f32[16,768]{1,0:T(8,128)S(1)} custom-call(bf16[3072,768]{1,0:T(8,128)(2,1)S(1)} %bitcast.13, bf16[24,768]{1,0:T(8,128)(2,1)S(1)} %get-tuple-element.27.refs_0_.refs_3_, bf16[24,768]{1,0:T(8,128)(2,1)S(1)} %collective-permute-done.6.refs_1_), custom_call_target="tpu_custom_call" | custom-call | flops 1000000000 | bytes 1048576 | tf_op jit(solution)/shard_map/pallas_call | solution.py:213
  17.4 0.4 %collective-permute-done.5.refs_0_ = bf16[24,768]{1,0:T(8,128)(2,1)S(1)} collective-permute-done((bf16[24,768]{1,0:T(8,128)(2,1)S(1)}, bf16[24,768]{1,0:T(8,128)(2,1)S(1)}, u32[]{:S(2)}, u32[]{:S(2)}) %collective-permute-start.5) | collective-permute-done | bytes 36896 | tf_op jit(solution)/shard_map/ppermute | solution.py:241
  17.8 0.3 shard_map.101.total_ref
  18.1 0.1 collective-permute-done.7.attention_ref.refs_2_
  18.2 0.3 shard_map.102
  18.5 5.8 %collective-permute-start.8 = (bf16[4,768]{1,0:T(4,128)(2,1)S(1)}, bf16[4,768]{1,0:T(4,128)(2,1)S(1)}, u32[]{:S(2)}, u32[]{:S(2)}) collective-permute-start(bf16[4,768]{1,0:T(4,128)(2,1)S(1)} %get-tuple-element.30), channel_id=1, source_target_pairs={{0,9},{1,2},{2,11},{3,0},{4,1},{5,6},{6,3},{7,4},{8,13},{9,14},{10... | collective-permute-start | bytes 18440 | tf_op jit(solution)/shard_map/ppermute | solution.py:250
  24.3 1.6 %collective-permute-start.9 = (bf16[4,768]{1,0:T(4,128)(2,1)S(1)}, bf16[4,768]{1,0:T(4,128)(2,1)S(1)}, u32[]{:S(2)}, u32[]{:S(2)}) collective-permute-start(bf16[4,768]{1,0:T(4,128)(2,1)S(1)} %get-tuple-element.31), channel_id=1, source_target_pairs={{0,5},{1,14},{2,7},{3,12},{4,13},{5,2},{6,15},{7,0},{8,1},{9,10},{... | collective-permute-start | bytes 18440 | tf_op jit(solution)/shard_map/ppermute | solution.py:250
  25.9 1.0 %collective-permute-start.10 = (bf16[4,768]{1,0:T(4,128)(2,1)S(1)}, bf16[4,768]{1,0:T(4,128)(2,1)S(1)}, u32[]{:S(2)}, u32[]{:S(2)}) collective-permute-start(bf16[4,768]{1,0:T(4,128)(2,1)S(1)} %get-tuple-element.32), channel_id=1, source_target_pairs={{0,1},{1,10},{2,3},{3,8},{4,5},{5,14},{6,7},{7,12},{8,9},{9,6},{10... | collective-permute-start | bytes 18440 | tf_op jit(solution)/shard_map/ppermute | solution.py:250
  27.0 0.0 collective-permute-start.11
  27.0 0.7 %shard_map.104 = bf16[1,4,2,3072]{3,2,1,0:T(2,128)(2,1)} custom-call(bf16[24,768]{1,0:T(8,128)(2,1)S(1)} %collective-permute-done.5.refs_0_, bf16[24,768]{1,0:T(8,128)(2,1)S(1)} %collective-permute-done.6.refs_1_, bf16[24,768]{1,0:T(8,128)(2,1)S(1)} %collective-permute-done.7.attention_ref.refs_2_, bf16[24,768]{1,0:T(8,128)(2,1)S(1)} %get-tuple-element.27.refs_0_.refs_3_), custom_call_target="tpu_custom_call" | custom-call | flops 1000000000 | bytes 1048576 | tf_op jit(solution)/shard_map/pallas_call | solution.py:213
  27.7 0.0 collective-permute-done.8.refs_0_
  27.7 0.6 %collective-permute-done.9.refs_1_ = bf16[4,768]{1,0:T(4,128)(2,1)S(1)} collective-permute-done((bf16[4,768]{1,0:T(4,128)(2,1)S(1)}, bf16[4,768]{1,0:T(4,128)(2,1)S(1)}, u32[]{:S(2)}, u32[]{:S(2)}) %collective-permute-start.9) | collective-permute-done | bytes 6176 | tf_op jit(solution)/shard_map/ppermute | solution.py:250
  28.3 0.0 collective-permute-done.10.refs_2_
  28.3 3.5 %collective-permute-done.11.refs_3_ = bf16[4,768]{1,0:T(4,128)(2,1)S(1)} collective-permute-done((bf16[4,768]{1,0:T(4,128)(2,1)S(1)}, bf16[4,768]{1,0:T(4,128)(2,1)S(1)}, u32[]{:S(2)}, u32[]{:S(2)}) %collective-permute-start.11) | collective-permute-done | bytes 6176 | tf_op jit(solution)/shard_map/ppermute | solution.py:250
  31.8 0.6 %shard_map.103 = bf16[1,4,3072]{2,1,0:T(4,128)(2,1)} custom-call(bf16[4,768]{1,0:T(4,128)(2,1)S(1)} %collective-permute-done.8.refs_0_, bf16[4,768]{1,0:T(4,128)(2,1)S(1)} %collective-permute-done.9.refs_1_, bf16[4,768]{1,0:T(4,128)(2,1)S(1)} %collective-permute-done.10.refs_2_, bf16[4,768]{1,0:T(4,128)(2,1)S(1)} %collective-permute-done.11.refs_3_), custom_call_target="tpu_custom_call" | custom-call | flops 1000000000 | bytes 1048576 | tf_op jit(solution)/shard_map/pallas_call | solution.py:213
  (12 shorter events, 0.0 us)
Async XLA Ops:
  0.6 4.5 %copy-start.1 = (bf16[1,4,3072]{2,1,0:T(4,128)(2,1)S(1)}, bf16[1,4,3072]{2,1,0:T(4,128)(2,1)}, u32[]{:S(2)}) copy-start(bf16[1,4,3072]{2,1,0:T(4,128)(2,1)} %param.8) | copy-start | bytes 73732
  0.6 4.5 %copy-start.4 = (bf16[1,4,4,2,3072]{4,3,2,1,0:T(2,128)(2,1)S(1)}, bf16[1,4,4,2,3072]{4,3,2,1,0:T(2,128)(2,1)}, u32[]{:S(2)}) copy-start(bf16[1,4,4,2,3072]{4,3,2,1,0:T(2,128)(2,1)} %cache_ref.3) | copy-start | bytes 589828
  0.6 4.5 %copy-start.5 = (s32[4]{0:T(128)S(1)}, s32[4]{0:T(128)}, u32[]{:S(2)}) copy-start(s32[4]{0:T(128)} %param.14) | copy-start | bytes 52
  0.7 8.6 %collective-permute-start.2 = (bf16[4,3072]{1,0:T(4,128)(2,1)}, bf16[4,3072]{1,0:T(4,128)(2,1)S(1)}, u32[]{:S(2)}, u32[]{:S(2)}) collective-permute-start(bf16[4,3072]{1,0:T(4,128)(2,1)} %bitcast.20), channel_id=1, source_target_pairs={{0,4},{4,0},{8,12},{12,8},{1,5},{5,1},{9,13},{13,9},{2,6},{6,2},{1... | collective-permute-start | bytes 73736 | tf_op jit(solution)/shard_map/ppermute | solution.py:241
  2.8 6.4 %collective-permute-start.1 = (bf16[4,3072]{1,0:T(4,128)(2,1)}, bf16[4,3072]{1,0:T(4,128)(2,1)S(1)}, u32[]{:S(2)}, u32[]{:S(2)}) collective-permute-start(bf16[4,3072]{1,0:T(4,128)(2,1)} %bitcast.21), channel_id=1, source_target_pairs={{0,8},{4,12},{8,0},{12,4},{1,9},{5,13},{9,1},{13,5},{2,10},{6,14},... | collective-permute-start | bytes 73736 | tf_op jit(solution)/shard_map/ppermute | solution.py:241
  5.2 5.3 %slice-start.2 = ((s8[14155776]{0:T(1024)(128)(4,1)}), s8[4194304]{0:T(1024)(128)(4,1)S(1)}, s32[]{:S(2)}) async-start(s8[14155776]{0:T(1024)(128)(4,1)} %bitcast.16), calls=%async_computation.2 | async-start | bytes 8388608
  5.2 5.3 %slice-start.3 = ((s8[14155776]{0:T(1024)(128)(4,1)}), s8[4194304]{0:T(1024)(128)(4,1)S(1)}, s32[]{:S(2)}) async-start(s8[14155776]{0:T(1024)(128)(4,1)} %bitcast.16), calls=%async_computation.3 | async-start | bytes 8388608
  5.2 5.2 %copy-start = (f32[1,4,3,3072]{3,1,2,0:T(4,128)S(1)}, f32[1,4,3,3072]{3,1,2,0:T(4,128)}, u32[]{:S(2)}) copy-start(f32[1,4,3,3072]{3,1,2,0:T(4,128)} %param.13) | copy-start | bytes 442372
  5.2 5.2 %copy-start.2 = (f32[1,2,128]{2,1,0:T(2,128)S(1)}, f32[1,2,128]{2,1,0:T(2,128)}, u32[]{:S(2)}) copy-start(f32[1,2,128]{2,1,0:T(2,128)} %param.12) | copy-start | bytes 3076
  5.2 5.2 %copy-start.3 = (s32[4]{0:T(128)S(1)}, s32[4]{0:T(128)}, u32[]{:S(2)}) copy-start(s32[4]{0:T(128)} %param.15) | copy-start | bytes 52
  5.3 5.1 %slice-start.4 = ((s8[14155776]{0:T(1024)(128)(4,1)}), s8[4194304]{0:T(1024)(128)(4,1)S(1)}, s32[]{:S(2)}) async-start(s8[14155776]{0:T(1024)(128)(4,1)} %bitcast.16), calls=%async_computation.4 | async-start | bytes 8388608
  5.4 5.1 %slice-start.5 = ((s8[14155776]{0:T(1024)(128)(4,1)}), s8[1572864]{0:T(1024)(128)(4,1)S(1)}, s32[]{:S(2)}) async-start(s8[14155776]{0:T(1024)(128)(4,1)} %bitcast.16), calls=%async_computation.5 | async-start | bytes 3145728
  5.4 5.1 %collective-permute-start = (bf16[40,768]{1,0:T(8,128)(2,1)S(1)}, bf16[40,768]{1,0:T(8,128)(2,1)S(1)}, u32[]{:S(2)}, u32[]{:S(2)}) collective-permute-start(bf16[40,768]{1,0:T(8,128)(2,1)S(1)} %shard_map.96), channel_id=1, source_target_pairs={{0,12},{4,8},{8,4},{12,0},{1,13},{5,9},{9,5},{13,1},{2,14},{6,10},... | collective-permute-start | bytes 184328 | tf_op jit(solution)/shard_map/ppermute | solution.py:241
  6.2 10.8 %slice-start = ((s8[4718592]{0:T(1024)(128)(4,1)}), s8[4194304]{0:T(1024)(128)(4,1)S(1)}, s32[]{:S(2)}) async-start(s8[4718592]{0:T(1024)(128)(4,1)} %bitcast.11), calls=%async_computation | async-start | bytes 8388608
  6.2 6.5 %collective-permute-start.3 = (bf16[24,768]{1,0:T(8,128)(2,1)S(1)}, bf16[24,768]{1,0:T(8,128)(2,1)S(1)}, u32[]{:S(2)}, u32[]{:S(2)}) collective-permute-start(bf16[24,768]{1,0:T(8,128)(2,1)S(1)} %get-tuple-element.23), channel_id=1, source_target_pairs={{0,8},{4,12},{8,0},{12,4},{1,9},{5,13},{9,1},{13,5},{2,10},{6,14},... | collective-permute-start | bytes 110600 | tf_op jit(solution)/shard_map/ppermute | solution.py:241
  7.1 5.6 %collective-permute-start.4 = (bf16[24,768]{1,0:T(8,128)(2,1)S(1)}, bf16[24,768]{1,0:T(8,128)(2,1)S(1)}, u32[]{:S(2)}, u32[]{:S(2)}) collective-permute-start(bf16[24,768]{1,0:T(8,128)(2,1)S(1)} %get-tuple-element.24), channel_id=1, source_target_pairs={{0,4},{4,0},{8,12},{12,8},{1,5},{5,1},{9,13},{13,9},{2,6},{6,2},{1... | collective-permute-start | bytes 110600 | tf_op jit(solution)/shard_map/ppermute | solution.py:241
  10.5 6.5 %slice-start.1 = ((s8[4718592]{0:T(1024)(128)(4,1)}), s8[524288]{0:T(1024)(128)(4,1)S(1)}, s32[]{:S(2)}) async-start(s8[4718592]{0:T(1024)(128)(4,1)} %bitcast.11), calls=%async_computation.1 | async-start | bytes 1048576
  13.1 3.9 %collective-permute-start.6 = (bf16[24,768]{1,0:T(8,128)(2,1)S(1)}, bf16[24,768]{1,0:T(8,128)(2,1)S(1)}, u32[]{:S(2)}, u32[]{:S(2)}) collective-permute-start(bf16[24,768]{1,0:T(8,128)(2,1)S(1)} %get-tuple-element.28), channel_id=1, source_target_pairs={{0,8},{4,12},{8,0},{12,4},{1,9},{5,13},{9,1},{13,5},{2,10},{6,14},... | collective-permute-start | bytes 110600 | tf_op jit(solution)/shard_map/ppermute | solution.py:241
  13.2 4.7 %collective-permute-start.5 = (bf16[24,768]{1,0:T(8,128)(2,1)S(1)}, bf16[24,768]{1,0:T(8,128)(2,1)S(1)}, u32[]{:S(2)}, u32[]{:S(2)}) collective-permute-start(bf16[24,768]{1,0:T(8,128)(2,1)S(1)} %get-tuple-element.26), channel_id=1, source_target_pairs={{0,12},{4,8},{8,4},{12,0},{1,13},{5,9},{9,5},{13,1},{2,14},{6,10},... | collective-permute-start | bytes 110600 | tf_op jit(solution)/shard_map/ppermute | solution.py:241
  15.3 3.0 %collective-permute-start.7 = (bf16[24,768]{1,0:T(8,128)(2,1)S(1)}, bf16[24,768]{1,0:T(8,128)(2,1)S(1)}, u32[]{:S(2)}, u32[]{:S(2)}) collective-permute-start(bf16[24,768]{1,0:T(8,128)(2,1)S(1)} %get-tuple-element.29), channel_id=1, source_target_pairs={{0,4},{4,0},{8,12},{12,8},{1,5},{5,1},{9,13},{13,9},{2,6},{6,2},{1... | collective-permute-start | bytes 110600 | tf_op jit(solution)/shard_map/ppermute | solution.py:241
  18.5 9.1 %collective-permute-start.8 = (bf16[4,768]{1,0:T(4,128)(2,1)S(1)}, bf16[4,768]{1,0:T(4,128)(2,1)S(1)}, u32[]{:S(2)}, u32[]{:S(2)}) collective-permute-start(bf16[4,768]{1,0:T(4,128)(2,1)S(1)} %get-tuple-element.30), channel_id=1, source_target_pairs={{0,9},{1,2},{2,11},{3,0},{4,1},{5,6},{6,3},{7,4},{8,13},{9,14},{10... | collective-permute-start | bytes 18440 | tf_op jit(solution)/shard_map/ppermute | solution.py:250
  24.3 4.0 %collective-permute-start.9 = (bf16[4,768]{1,0:T(4,128)(2,1)S(1)}, bf16[4,768]{1,0:T(4,128)(2,1)S(1)}, u32[]{:S(2)}, u32[]{:S(2)}) collective-permute-start(bf16[4,768]{1,0:T(4,128)(2,1)S(1)} %get-tuple-element.31), channel_id=1, source_target_pairs={{0,5},{1,14},{2,7},{3,12},{4,13},{5,2},{6,15},{7,0},{8,1},{9,10},{... | collective-permute-start | bytes 18440 | tf_op jit(solution)/shard_map/ppermute | solution.py:250
  25.9 2.4 %collective-permute-start.10 = (bf16[4,768]{1,0:T(4,128)(2,1)S(1)}, bf16[4,768]{1,0:T(4,128)(2,1)S(1)}, u32[]{:S(2)}, u32[]{:S(2)}) collective-permute-start(bf16[4,768]{1,0:T(4,128)(2,1)S(1)} %get-tuple-element.32), channel_id=1, source_target_pairs={{0,1},{1,10},{2,3},{3,8},{4,5},{5,14},{6,7},{7,12},{8,9},{9,6},{10... | collective-permute-start | bytes 18440 | tf_op jit(solution)/shard_map/ppermute | solution.py:250
  27.0 4.9 %collective-permute-start.11 = (bf16[4,768]{1,0:T(4,128)(2,1)S(1)}, bf16[4,768]{1,0:T(4,128)(2,1)S(1)}, u32[]{:S(2)}, u32[]{:S(2)}) collective-permute-start(bf16[4,768]{1,0:T(4,128)(2,1)S(1)} %get-tuple-element.33), channel_id=1, source_target_pairs={{0,13},{1,6},{2,15},{3,4},{4,9},{5,10},{6,11},{7,8},{8,5},{9,2},{1... | collective-permute-start | bytes 18440 | tf_op jit(solution)/shard_map/ppermute | solution.py:250

commit v3 on v1

--- a/solution.py
+++ b/solution.py
@@ -73,7 +73,7 @@
 
 def project_kernel(step_ref, mod_ref, gain_ref, weight_ref, *refs, slots, tokens, heads, size, stale):
     hidden_refs = refs[:slots][::-1]
-    q_ref, k_ref, normed_ref, held_ref, gate_ref, scratch = refs[slots:]
+    q_ref, k_ref, v_ref, held_ref, gate_ref, scratch = refs[slots:]
     mine = lax.axis_index("seq")
     columns, length = heads * size, slots * tokens
     step = lax.broadcasted_iota(jnp.int32, (mod_ref.shape[1], 1), 0).astype(F32) == entry(step_ref)
@@ -88,20 +88,20 @@
             rows.append(jnp.concatenate([cut[c * tokens : (c + 1) * tokens] for c in range(slots)], axis=1))
     rows = jnp.concatenate(rows, axis=0)
     normed = (layer_norm(rows) * (1.0 + modulate[1]) + modulate[0]).astype(BF16)
-    normed_ref[...] = normed
     for part, out in enumerate((q_ref, k_ref)):
         dotted = jnp.dot(normed, weight_ref[part], preferred_element_type=F32).astype(BF16).astype(F32)
         stacked = jnp.concatenate([dotted[:, h * size : (h + 1) * size] for h in range(heads)], axis=0)
         stacked = head_norm(stacked, gain_ref[pl.ds(part, 1), :]).astype(BF16)
         for h in range(heads):
             out[:, h * size : (h + 1) * size] = stacked[h * length : (h + 1) * length]
+    v_ref[...] = jnp.dot(normed, weight_ref[2], preferred_element_type=F32).astype(BF16)
     scratch[...] = rows
     held_ref[...] = scratch[:, pl.ds(start, columns)].astype(BF16)
     gates = jnp.where(step, mod_ref[2, :, pl.ds(start, columns)], 0.0)
     gate_ref[...] = jnp.sum(gates, axis=0, keepdims=True)
 
 
-def attend_kernel(q_ref, k_ref, normed_ref, weight_ref, *refs, slots, tokens, stale, heads, size):
+def attend_kernel(q_ref, k_ref, v_ref, *refs, slots, tokens, stale, heads, size):
     old, outs = refs[:slots][::-1], refs[slots:]
     old = [r[: 2 * stale].astype(F32) for r in old]
     fresh_keys = k_ref[...].astype(F32)
@@ -114,7 +114,7 @@
     cuts = [slice(h * size, (h + 1) * size) for h in range(heads)]
     dims = (((1,), (1,)), ((), ()))
     scores = [lax.dot_general(queries[:, cut], keys[:, cut], dims, preferred_element_type=F32) for cut in cuts]
-    fresh_values = jnp.dot(normed_ref[...], weight_ref[2], preferred_element_type=F32).astype(BF16).astype(F32)
+    fresh_values = v_ref[...].astype(F32)
     scores = jnp.concatenate(scores, axis=0) / math.sqrt(size)
     top = jnp.max(scores, axis=-1, keepdims=True)
     weights = jnp.exp(scores - top).astype(BF16).astype(F32)
@@ -249,7 +249,7 @@
 
     own = hidden[0]
     alone = {b: moved(own, b) for b in split}
-    ahead = call(ahead_kernel, 5e9, array(8, 128, dtype=F32), [])
+    ahead = call(ahead_kernel, 2e10, array(8, 128, dtype=F32), [])
     packed = {}
     far = tuple(b for b in range(1, slots) if b not in split)
     for numbers in (far, (0, *split)):
@@ -269,13 +269,13 @@
     old = exchanged(packed)
     inputs = [own] + [alone[b] if b in split else old[b] for b in range(1, slots)]
     weights = jnp.transpose(w_qkv[0], (1, 0, 2))
-    queries, keys, normed, held, gate = call(
+    queries, keys, values, held, gate = call(
         project_kernel,
         2e9,
         [
             array(rows, columns),
             array(rows, columns),
-            array(rows, width),
+            array(rows, columns),
             array(rows, columns),
             array(1, columns, dtype=F32),
         ],
@@ -291,7 +291,7 @@
         attend_kernel,
         2e9,
         [array(rows + 2 * tokens, columns)] * slots,
-        [queries, keys, normed, weights, *old[::-1]],
+        [queries, keys, values, *old[::-1]],
         slots=slots,
         tokens=tokens,
         stale=stale,
@@ -300,7 +300,7 @@
     )
     attention = exchanged(ordered)
     out_weights = w_out[0]
-    groups = [(0, 2), (3,)]
+    groups = [(0, 2), (3,)] if slots == 4 else [(0,)] + [(b,) for b in range(slots - 1, 1, -1)]
     total = []
     for numbers in groups:
         operands = [out_weights] + [attention[b] for b in numbers] + total

time: 32.7 us -> 32.6 us (level)
  transfers between devices with their start and end apart: 12 -> 12, of which waited for: 6 -> 6; matrix products, arithmetic and copies ran while one was open for 0% -> 0% of each run, Pallas kernels for 10% -> 12%
where the time goes in v3:
time: 32.6 us; the launch traced here: 32.4 us
  starting transfers between devices  19.3 us (59%)
  waiting for transfers between devices  7.05 us (22%)
  Pallas kernels  5.18 us (16%)
  between operations  0.82 us (3%)
    ppermute x8, starting transfers between devices, moved(): return lax.ppermute(array, 'seq', [(j, j ^ number) for j in range(slots)])  10.9 us
    ppermute x4, starting transfers between devices, onward(): return lax.ppermute(array, ('seq', 'section'), pairs)  8.43 us
    pallas_call x10, Pallas kernels, call(): pl.pallas_call(functools.partial(kernel, **sizes), out_shape=out_shape, i...  5.18 us
    ppermute x4, waiting for transfers between devices, onward(): return lax.ppermute(array, ('seq', 'section'), pairs)  4.14 us
    ppermute x8, waiting for transfers between devices, moved(): return lax.ppermute(array, 'seq', [(j, j ^ number) for j in range(slots)])  2.91 us
  transfers between devices with their start and end apart: 12, of which 6 were waited for; matrix products, arithmetic and copies ran while one was open for 0% of the time, Pallas kernels for 12%

profile of v3, /device:TPU:1, one launch (start us, length us, event | category | flops | bytes accessed | tf_op | source)
XLA Modules:
  0.0 32.4 jit_solution(4907267855885174024)
XLA Ops:
  0.6 0.0 copy-start.1
  0.6 0.0 copy-start.4
  0.6 0.0 copy-start.5
  0.7 2.2 %collective-permute-start.2 = (bf16[4,3072]{1,0:T(4,128)(2,1)}, bf16[4,3072]{1,0:T(4,128)(2,1)S(1)}, u32[]{:S(2)}, u32[]{:S(2)}) collective-permute-start(bf16[4,3072]{1,0:T(4,128)(2,1)} %bitcast.20), channel_id=1, source_target_pairs={{0,4},{4,0},{8,12},{12,8},{1,5},{5,1},{9,13},{13,9},{2,6},{6,2},{1... | collective-permute-start | bytes 73736 | tf_op jit(solution)/shard_map/ppermute | solution.py:236
  2.8 2.3 %collective-permute-start.1 = (bf16[4,3072]{1,0:T(4,128)(2,1)}, bf16[4,3072]{1,0:T(4,128)(2,1)S(1)}, u32[]{:S(2)}, u32[]{:S(2)}) collective-permute-start(bf16[4,3072]{1,0:T(4,128)(2,1)} %bitcast.21), channel_id=1, source_target_pairs={{0,8},{4,12},{8,0},{12,4},{1,9},{5,13},{9,1},{13,5},{2,10},{6,14},... | collective-permute-start | bytes 73736 | tf_op jit(solution)/shard_map/ppermute | solution.py:236
  5.2 0.0 copy-done.5
  5.2 0.0 slice-start.2
  5.2 0.0 slice-start.3
  5.2 0.0 copy-start
  5.2 0.0 copy-start.2
  5.2 0.0 copy-start.3
  5.2 0.1 shard_map.96
  5.3 0.0 slice-start.4
  5.4 0.0 slice-start.5
  5.4 0.6 %collective-permute-start = (bf16[40,768]{1,0:T(8,128)(2,1)S(1)}, bf16[40,768]{1,0:T(8,128)(2,1)S(1)}, u32[]{:S(2)}, u32[]{:S(2)}) collective-permute-start(bf16[40,768]{1,0:T(8,128)(2,1)S(1)} %shard_map.96), channel_id=1, source_target_pairs={{0,12},{4,8},{8,4},{12,0},{1,13},{5,9},{9,5},{13,1},{2,14},{6,10},... | collective-permute-start | bytes 184328 | tf_op jit(solution)/shard_map/ppermute | solution.py:236
  6.0 0.2 shard_map.98
  6.2 0.0 slice-start
  6.2 0.9 %collective-permute-start.3 = (bf16[24,768]{1,0:T(8,128)(2,1)S(1)}, bf16[24,768]{1,0:T(8,128)(2,1)S(1)}, u32[]{:S(2)}, u32[]{:S(2)}) collective-permute-start(bf16[24,768]{1,0:T(8,128)(2,1)S(1)} %get-tuple-element.23), channel_id=1, source_target_pairs={{0,8},{4,12},{8,0},{12,4},{1,9},{5,13},{9,1},{13,5},{2,10},{6,14},... | collective-permute-start | bytes 110600 | tf_op jit(solution)/shard_map/ppermute | solution.py:236
  7.1 2.2 %collective-permute-start.4 = (bf16[24,768]{1,0:T(8,128)(2,1)S(1)}, bf16[24,768]{1,0:T(8,128)(2,1)S(1)}, u32[]{:S(2)}, u32[]{:S(2)}) collective-permute-start(bf16[24,768]{1,0:T(8,128)(2,1)S(1)} %get-tuple-element.24), channel_id=1, source_target_pairs={{0,4},{4,0},{8,12},{12,8},{1,5},{5,1},{9,13},{13,9},{2,6},{6,2},{1... | collective-permute-start | bytes 110600 | tf_op jit(solution)/shard_map/ppermute | solution.py:236
  9.3 0.0 collective-permute-done.2.refs_2_
  9.3 0.0 collective-permute-done.1.refs_1_
  9.3 1.2 %collective-permute-done.refs_0_ = bf16[40,768]{1,0:T(8,128)(2,1)S(1)} collective-permute-done((bf16[40,768]{1,0:T(8,128)(2,1)S(1)}, bf16[40,768]{1,0:T(8,128)(2,1)S(1)}, u32[]{:S(2)}, u32[]{:S(2)}) %collective-permute-start) | collective-permute-done | bytes 61472 | tf_op jit(solution)/shard_map/ppermute | solution.py:236
  10.4 0.0 copy-done
  10.4 0.0 copy-done.2
  10.5 0.0 slice-start.1
  10.5 2.1 %shard_map.97 = (bf16[16,768]{1,0:T(8,128)(2,1)S(1)}, bf16[16,768]{1,0:T(8,128)(2,1)S(1)}, bf16[16,768]{1,0:T(8,128)(2,1)S(1)}, bf16[16,768]{1,0:T(8,128)(2,1)S(1)}, f32[1,768]{1,0:T(1,128)S(1)}) custom-call(s32[1,4]{1,0:T(1,128)S(1)} %bitcast.26, f32[3,4,3072]{2,1,0:T(4,128)S(1)} %bitcast.19, f32[2,128]{1,0:T(2,128)S(1)} %bitcast.25, ...), custom_call_target="tpu_custom_call" | custom-call | flops 2000000000 | bytes 1048576 | tf_op jit(solution)/shard_map/pallas_call | solution.py:208
  12.6 0.0 collective-permute-done.3.refs_1_
  12.6 0.0 collective-permute-done.4.refs_2_
  12.7 0.4 %shard_map.99 = (bf16[24,768]{1,0:T(8,128)(2,1)S(1)}, bf16[24,768]{1,0:T(8,128)(2,1)S(1)}, bf16[24,768]{1,0:T(8,128)(2,1)S(1)}, bf16[24,768]{1,0:T(8,128)(2,1)S(1)}) custom-call(bf16[16,768]{1,0:T(8,128)(2,1)S(1)} %get-tuple-element.20.q_ref, bf16[16,768]{1,0:T(8,128)(2,1)S(1)} %get-tuple-element.21.k_ref, bf16[16,768]{1,0:T(8,128)(2,1)S(1)} %get-tuple-element.22.v_ref, ...), custom_call_target="tpu_custom_call" | custom-call | flops 2000000000 | bytes 1048576 | tf_op jit(solution)/shard_map/pallas_call | solution.py:208
  13.1 0.1 collective-permute-start.6
  13.2 2.1 %collective-permute-start.5 = (bf16[24,768]{1,0:T(8,128)(2,1)S(1)}, bf16[24,768]{1,0:T(8,128)(2,1)S(1)}, u32[]{:S(2)}, u32[]{:S(2)}) collective-permute-start(bf16[24,768]{1,0:T(8,128)(2,1)S(1)} %get-tuple-element.26), channel_id=1, source_target_pairs={{0,12},{4,8},{8,4},{12,0},{1,13},{5,9},{9,5},{13,1},{2,14},{6,10},... | collective-permute-start | bytes 110600 | tf_op jit(solution)/shard_map/ppermute | solution.py:236
  15.3 0.5 %collective-permute-start.7 = (bf16[24,768]{1,0:T(8,128)(2,1)S(1)}, bf16[24,768]{1,0:T(8,128)(2,1)S(1)}, u32[]{:S(2)}, u32[]{:S(2)}) collective-permute-start(bf16[24,768]{1,0:T(8,128)(2,1)S(1)} %get-tuple-element.29), channel_id=1, source_target_pairs={{0,4},{4,0},{8,12},{12,8},{1,5},{5,1},{9,13},{13,9},{2,6},{6,2},{1... | collective-permute-start | bytes 110600 | tf_op jit(solution)/shard_map/ppermute | solution.py:236
  15.8 1.2 %collective-permute-done.6.refs_1_ = bf16[24,768]{1,0:T(8,128)(2,1)S(1)} collective-permute-done((bf16[24,768]{1,0:T(8,128)(2,1)S(1)}, bf16[24,768]{1,0:T(8,128)(2,1)S(1)}, u32[]{:S(2)}, u32[]{:S(2)}) %collective-permute-start.6) | collective-permute-done | bytes 36896 | tf_op jit(solution)/shard_map/ppermute | solution.py:236
  17.0 0.4 %shard_map.100.refs_1_ = f32[16,768]{1,0:T(8,128)S(1)} custom-call(bf16[3072,768]{1,0:T(8,128)(2,1)S(1)} %bitcast.13, bf16[24,768]{1,0:T(8,128)(2,1)S(1)} %get-tuple-element.27.refs_0_.refs_3_, bf16[24,768]{1,0:T(8,128)(2,1)S(1)} %collective-permute-done.6.refs_1_), custom_call_target="tpu_custom_call" | custom-call | flops 1000000000 | bytes 1048576 | tf_op jit(solution)/shard_map/pallas_call | solution.py:208
  17.4 0.4 %collective-permute-done.5.refs_0_ = bf16[24,768]{1,0:T(8,128)(2,1)S(1)} collective-permute-done((bf16[24,768]{1,0:T(8,128)(2,1)S(1)}, bf16[24,768]{1,0:T(8,128)(2,1)S(1)}, u32[]{:S(2)}, u32[]{:S(2)}) %collective-permute-start.5) | collective-permute-done | bytes 36896 | tf_op jit(solution)/shard_map/ppermute | solution.py:236
  17.8 0.3 shard_map.101.total_ref
  18.1 0.1 collective-permute-done.7.attention_ref.refs_2_
  18.2 0.3 shard_map.102
  18.5 5.8 %collective-permute-start.8 = (bf16[4,768]{1,0:T(4,128)(2,1)S(1)}, bf16[4,768]{1,0:T(4,128)(2,1)S(1)}, u32[]{:S(2)}, u32[]{:S(2)}) collective-permute-start(bf16[4,768]{1,0:T(4,128)(2,1)S(1)} %get-tuple-element.30), channel_id=1, source_target_pairs={{0,9},{1,2},{2,11},{3,0},{4,1},{5,6},{6,3},{7,4},{8,13},{9,14},{10... | collective-permute-start | bytes 18440 | tf_op jit(solution)/shard_map/ppermute | solution.py:245
  24.3 1.6 %collective-permute-start.9 = (bf16[4,768]{1,0:T(4,128)(2,1)S(1)}, bf16[4,768]{1,0:T(4,128)(2,1)S(1)}, u32[]{:S(2)}, u32[]{:S(2)}) collective-permute-start(bf16[4,768]{1,0:T(4,128)(2,1)S(1)} %get-tuple-element.31), channel_id=1, source_target_pairs={{0,5},{1,14},{2,7},{3,12},{4,13},{5,2},{6,15},{7,0},{8,1},{9,10},{... | collective-permute-start | bytes 18440 | tf_op jit(solution)/shard_map/ppermute | solution.py:245
  25.9 1.0 %collective-permute-start.10 = (bf16[4,768]{1,0:T(4,128)(2,1)S(1)}, bf16[4,768]{1,0:T(4,128)(2,1)S(1)}, u32[]{:S(2)}, u32[]{:S(2)}) collective-permute-start(bf16[4,768]{1,0:T(4,128)(2,1)S(1)} %get-tuple-element.32), channel_id=1, source_target_pairs={{0,1},{1,10},{2,3},{3,8},{4,5},{5,14},{6,7},{7,12},{8,9},{9,6},{10... | collective-permute-start | bytes 18440 | tf_op jit(solution)/shard_map/ppermute | solution.py:245
  27.0 0.0 collective-permute-start.11
  27.0 0.7 %shard_map.104 = bf16[1,4,2,3072]{3,2,1,0:T(2,128)(2,1)} custom-call(bf16[24,768]{1,0:T(8,128)(2,1)S(1)} %collective-permute-done.5.refs_0_, bf16[24,768]{1,0:T(8,128)(2,1)S(1)} %collective-permute-done.6.refs_1_, bf16[24,768]{1,0:T(8,128)(2,1)S(1)} %collective-permute-done.7.attention_ref.refs_2_, bf16[24,768]{1,0:T(8,128)(2,1)S(1)} %get-tuple-element.27.refs_0_.refs_3_), custom_call_target="tpu_custom_call" | custom-call | flops 1000000000 | bytes 1048576 | tf_op jit(solution)/shard_map/pallas_call | solution.py:208
  27.7 0.0 collective-permute-done.8.refs_0_
  27.7 0.6 %collective-permute-done.9.refs_1_ = bf16[4,768]{1,0:T(4,128)(2,1)S(1)} collective-permute-done((bf16[4,768]{1,0:T(4,128)(2,1)S(1)}, bf16[4,768]{1,0:T(4,128)(2,1)S(1)}, u32[]{:S(2)}, u32[]{:S(2)}) %collective-permute-start.9) | collective-permute-done | bytes 6176 | tf_op jit(solution)/shard_map/ppermute | solution.py:245
  28.3 0.0 collective-permute-done.10.refs_2_
  28.3 3.5 %collective-permute-done.11.refs_3_ = bf16[4,768]{1,0:T(4,128)(2,1)S(1)} collective-permute-done((bf16[4,768]{1,0:T(4,128)(2,1)S(1)}, bf16[4,768]{1,0:T(4,128)(2,1)S(1)}, u32[]{:S(2)}, u32[]{:S(2)}) %collective-permute-start.11) | collective-permute-done | bytes 6176 | tf_op jit(solution)/shard_map/ppermute | solution.py:245
  31.8 0.6 %shard_map.103 = bf16[1,4,3072]{2,1,0:T(4,128)(2,1)} custom-call(bf16[4,768]{1,0:T(4,128)(2,1)S(1)} %collective-permute-done.8.refs_0_, bf16[4,768]{1,0:T(4,128)(2,1)S(1)} %collective-permute-done.9.refs_1_, bf16[4,768]{1,0:T(4,128)(2,1)S(1)} %collective-permute-done.10.refs_2_, bf16[4,768]{1,0:T(4,128)(2,1)S(1)} %collective-permute-done.11.refs_3_), custom_call_target="tpu_custom_call" | custom-call | flops 1000000000 | bytes 1048576 | tf_op jit(solution)/shard_map/pallas_call | solution.py:208
  (12 shorter events, 0.0 us)
Async XLA Ops:
  0.6 4.5 %copy-start.1 = (bf16[1,4,3072]{2,1,0:T(4,128)(2,1)S(1)}, bf16[1,4,3072]{2,1,0:T(4,128)(2,1)}, u32[]{:S(2)}) copy-start(bf16[1,4,3072]{2,1,0:T(4,128)(2,1)} %param.8) | copy-start | bytes 73732
  0.6 4.5 %copy-start.4 = (bf16[1,4,4,2,3072]{4,3,2,1,0:T(2,128)(2,1)S(1)}, bf16[1,4,4,2,3072]{4,3,2,1,0:T(2,128)(2,1)}, u32[]{:S(2)}) copy-start(bf16[1,4,4,2,3072]{4,3,2,1,0:T(2,128)(2,1)} %cache_ref.3) | copy-start | bytes 589828
  0.6 4.5 %copy-start.5 = (s32[4]{0:T(128)S(1)}, s32[4]{0:T(128)}, u32[]{:S(2)}) copy-start(s32[4]{0:T(128)} %param.14) | copy-start | bytes 52
  0.7 8.6 %collective-permute-start.2 = (bf16[4,3072]{1,0:T(4,128)(2,1)}, bf16[4,3072]{1,0:T(4,128)(2,1)S(1)}, u32[]{:S(2)}, u32[]{:S(2)}) collective-permute-start(bf16[4,3072]{1,0:T(4,128)(2,1)} %bitcast.20), channel_id=1, source_target_pairs={{0,4},{4,0},{8,12},{12,8},{1,5},{5,1},{9,13},{13,9},{2,6},{6,2},{1... | collective-permute-start | bytes 73736 | tf_op jit(solution)/shard_map/ppermute | solution.py:236
  2.8 6.4 %collective-permute-start.1 = (bf16[4,3072]{1,0:T(4,128)(2,1)}, bf16[4,3072]{1,0:T(4,128)(2,1)S(1)}, u32[]{:S(2)}, u32[]{:S(2)}) collective-permute-start(bf16[4,3072]{1,0:T(4,128)(2,1)} %bitcast.21), channel_id=1, source_target_pairs={{0,8},{4,12},{8,0},{12,4},{1,9},{5,13},{9,1},{13,5},{2,10},{6,14},... | collective-permute-start | bytes 73736 | tf_op jit(solution)/shard_map/ppermute | solution.py:236
  5.2 5.3 %slice-start.2 = ((s8[14155776]{0:T(1024)(128)(4,1)}), s8[4194304]{0:T(1024)(128)(4,1)S(1)}, s32[]{:S(2)}) async-start(s8[14155776]{0:T(1024)(128)(4,1)} %bitcast.16), calls=%async_computation.2 | async-start | bytes 8388608
  5.2 5.3 %slice-start.3 = ((s8[14155776]{0:T(1024)(128)(4,1)}), s8[4194304]{0:T(1024)(128)(4,1)S(1)}, s32[]{:S(2)}) async-start(s8[14155776]{0:T(1024)(128)(4,1)} %bitcast.16), calls=%async_computation.3 | async-start | bytes 8388608
  5.2 5.2 %copy-start = (f32[1,4,3,3072]{3,1,2,0:T(4,128)S(1)}, f32[1,4,3,3072]{3,1,2,0:T(4,128)}, u32[]{:S(2)}) copy-start(f32[1,4,3,3072]{3,1,2,0:T(4,128)} %param.13) | copy-start | bytes 442372
  5.2 5.2 %copy-start.2 = (f32[1,2,128]{2,1,0:T(2,128)S(1)}, f32[1,2,128]{2,1,0:T(2,128)}, u32[]{:S(2)}) copy-start(f32[1,2,128]{2,1,0:T(2,128)} %param.12) | copy-start | bytes 3076
  5.2 5.2 %copy-start.3 = (s32[4]{0:T(128)S(1)}, s32[4]{0:T(128)}, u32[]{:S(2)}) copy-start(s32[4]{0:T(128)} %param.15) | copy-start | bytes 52
  5.3 5.1 %slice-start.4 = ((s8[14155776]{0:T(1024)(128)(4,1)}), s8[4194304]{0:T(1024)(128)(4,1)S(1)}, s32[]{:S(2)}) async-start(s8[14155776]{0:T(1024)(128)(4,1)} %bitcast.16), calls=%async_computation.4 | async-start | bytes 8388608
  5.4 5.1 %slice-start.5 = ((s8[14155776]{0:T(1024)(128)(4,1)}), s8[1572864]{0:T(1024)(128)(4,1)S(1)}, s32[]{:S(2)}) async-start(s8[14155776]{0:T(1024)(128)(4,1)} %bitcast.16), calls=%async_computation.5 | async-start | bytes 3145728
  5.4 5.1 %collective-permute-start = (bf16[40,768]{1,0:T(8,128)(2,1)S(1)}, bf16[40,768]{1,0:T(8,128)(2,1)S(1)}, u32[]{:S(2)}, u32[]{:S(2)}) collective-permute-start(bf16[40,768]{1,0:T(8,128)(2,1)S(1)} %shard_map.96), channel_id=1, source_target_pairs={{0,12},{4,8},{8,4},{12,0},{1,13},{5,9},{9,5},{13,1},{2,14},{6,10},... | collective-permute-start | bytes 184328 | tf_op jit(solution)/shard_map/ppermute | solution.py:236
  6.2 10.8 %slice-start = ((s8[4718592]{0:T(1024)(128)(4,1)}), s8[4194304]{0:T(1024)(128)(4,1)S(1)}, s32[]{:S(2)}) async-start(s8[4718592]{0:T(1024)(128)(4,1)} %bitcast.11), calls=%async_computation | async-start | bytes 8388608
  6.2 6.5 %collective-permute-start.3 = (bf16[24,768]{1,0:T(8,128)(2,1)S(1)}, bf16[24,768]{1,0:T(8,128)(2,1)S(1)}, u32[]{:S(2)}, u32[]{:S(2)}) collective-permute-start(bf16[24,768]{1,0:T(8,128)(2,1)S(1)} %get-tuple-element.23), channel_id=1, source_target_pairs={{0,8},{4,12},{8,0},{12,4},{1,9},{5,13},{9,1},{13,5},{2,10},{6,14},... | collective-permute-start | bytes 110600 | tf_op jit(solution)/shard_map/ppermute | solution.py:236
  7.1 5.6 %collective-permute-start.4 = (bf16[24,768]{1,0:T(8,128)(2,1)S(1)}, bf16[24,768]{1,0:T(8,128)(2,1)S(1)}, u32[]{:S(2)}, u32[]{:S(2)}) collective-permute-start(bf16[24,768]{1,0:T(8,128)(2,1)S(1)} %get-tuple-element.24), channel_id=1, source_target_pairs={{0,4},{4,0},{8,12},{12,8},{1,5},{5,1},{9,13},{13,9},{2,6},{6,2},{1... | collective-permute-start | bytes 110600 | tf_op jit(solution)/shard_map/ppermute | solution.py:236
  10.5 6.5 %slice-start.1 = ((s8[4718592]{0:T(1024)(128)(4,1)}), s8[524288]{0:T(1024)(128)(4,1)S(1)}, s32[]{:S(2)}) async-start(s8[4718592]{0:T(1024)(128)(4,1)} %bitcast.11), calls=%async_computation.1 | async-start | bytes 1048576
  13.1 3.9 %collective-permute-start.6 = (bf16[24,768]{1,0:T(8,128)(2,1)S(1)}, bf16[24,768]{1,0:T(8,128)(2,1)S(1)}, u32[]{:S(2)}, u32[]{:S(2)}) collective-permute-start(bf16[24,768]{1,0:T(8,128)(2,1)S(1)} %get-tuple-element.28), channel_id=1, source_target_pairs={{0,8},{4,12},{8,0},{12,4},{1,9},{5,13},{9,1},{13,5},{2,10},{6,14},... | collective-permute-start | bytes 110600 | tf_op jit(solution)/shard_map/ppermute | solution.py:236
  13.2 4.7 %collective-permute-start.5 = (bf16[24,768]{1,0:T(8,128)(2,1)S(1)}, bf16[24,768]{1,0:T(8,128)(2,1)S(1)}, u32[]{:S(2)}, u32[]{:S(2)}) collective-permute-start(bf16[24,768]{1,0:T(8,128)(2,1)S(1)} %get-tuple-element.26), channel_id=1, source_target_pairs={{0,12},{4,8},{8,4},{12,0},{1,13},{5,9},{9,5},{13,1},{2,14},{6,10},... | collective-permute-start | bytes 110600 | tf_op jit(solution)/shard_map/ppermute | solution.py:236
  15.3 3.0 %collective-permute-start.7 = (bf16[24,768]{1,0:T(8,128)(2,1)S(1)}, bf16[24,768]{1,0:T(8,128)(2,1)S(1)}, u32[]{:S(2)}, u32[]{:S(2)}) collective-permute-start(bf16[24,768]{1,0:T(8,128)(2,1)S(1)} %get-tuple-element.29), channel_id=1, source_target_pairs={{0,4},{4,0},{8,12},{12,8},{1,5},{5,1},{9,13},{13,9},{2,6},{6,2},{1... | collective-permute-start | bytes 110600 | tf_op jit(solution)/shard_map/ppermute | solution.py:236
  18.5 9.1 %collective-permute-start.8 = (bf16[4,768]{1,0:T(4,128)(2,1)S(1)}, bf16[4,768]{1,0:T(4,128)(2,1)S(1)}, u32[]{:S(2)}, u32[]{:S(2)}) collective-permute-start(bf16[4,768]{1,0:T(4,128)(2,1)S(1)} %get-tuple-element.30), channel_id=1, source_target_pairs={{0,9},{1,2},{2,11},{3,0},{4,1},{5,6},{6,3},{7,4},{8,13},{9,14},{10... | collective-permute-start | bytes 18440 | tf_op jit(solution)/shard_map/ppermute | solution.py:245
  24.3 4.0 %collective-permute-start.9 = (bf16[4,768]{1,0:T(4,128)(2,1)S(1)}, bf16[4,768]{1,0:T(4,128)(2,1)S(1)}, u32[]{:S(2)}, u32[]{:S(2)}) collective-permute-start(bf16[4,768]{1,0:T(4,128)(2,1)S(1)} %get-tuple-element.31), channel_id=1, source_target_pairs={{0,5},{1,14},{2,7},{3,12},{4,13},{5,2},{6,15},{7,0},{8,1},{9,10},{... | collective-permute-start | bytes 18440 | tf_op jit(solution)/shard_map/ppermute | solution.py:245
  25.9 2.4 %collective-permute-start.10 = (bf16[4,768]{1,0:T(4,128)(2,1)S(1)}, bf16[4,768]{1,0:T(4,128)(2,1)S(1)}, u32[]{:S(2)}, u32[]{:S(2)}) collective-permute-start(bf16[4,768]{1,0:T(4,128)(2,1)S(1)} %get-tuple-element.32), channel_id=1, source_target_pairs={{0,1},{1,10},{2,3},{3,8},{4,5},{5,14},{6,7},{7,12},{8,9},{9,6},{10... | collective-permute-start | bytes 18440 | tf_op jit(solution)/shard_map/ppermute | solution.py:245
  27.0 4.9 %collective-permute-start.11 = (bf16[4,768]{1,0:T(4,128)(2,1)S(1)}, bf16[4,768]{1,0:T(4,128)(2,1)S(1)}, u32[]{:S(2)}, u32[]{:S(2)}) collective-permute-start(bf16[4,768]{1,0:T(4,128)(2,1)S(1)} %get-tuple-element.33), channel_id=1, source_target_pairs={{0,13},{1,6},{2,15},{3,4},{4,9},{5,10},{6,11},{7,8},{8,5},{9,2},{1... | collective-permute-start | bytes 18440 | tf_op jit(solution)/shard_map/ppermute | solution.py:245

commit v4 on v3

--- a/solution.py
+++ b/solution.py
@@ -11,10 +11,10 @@
 
 APART = (1, 2)
 TURNS = (
-    ((3, 2, 1, 0), (1, 2, 0, 3)),
-    ((0, 1, 2, 3), (2, 3, 1, 0)),
-    ((1, 3, 0, 2), (3, 0, 2, 1)),
-    ((2, 0, 3, 1), (0, 1, 3, 2)),
+    ((2, 3, 1, 0), (1, 2, 0, 3)),
+    ((1, 0, 3, 2), (2, 3, 1, 0)),
+    ((0, 1, 2, 3), (0, 1, 3, 2)),
+    ((3, 2, 0, 1), (3, 0, 2, 1)),
 )
 
 F32 = jnp.float32
@@ -249,7 +249,7 @@
 
     own = hidden[0]
     alone = {b: moved(own, b) for b in split}
-    ahead = call(ahead_kernel, 2e10, array(8, 128, dtype=F32), [])
+    ahead = call(ahead_kernel, 5e9, array(8, 128, dtype=F32), [])
     packed = {}
     far = tuple(b for b in range(1, slots) if b not in split)
     for numbers in (far, (0, *split)):

time: 32.6 us -> 32.9 us (level)
  the two profiles are of different devices: /device:TPU:1 before, /device:TPU:0 now
where the time goes in v4:
time: 32.9 us; the launch traced here: 32.7 us
  starting transfers between devices  18 us (55%)
  waiting for transfers between devices  8.61 us (26%)
  Pallas kernels  5.18 us (16%)
  between operations  0.82 us (2%)
    ppermute x8, starting transfers between devices, moved(): return lax.ppermute(array, 'seq', [(j, j ^ number) for j in range(slots)])  13.8 us
    pallas_call x10, Pallas kernels, call(): pl.pallas_call(functools.partial(kernel, **sizes), out_shape=out_shape, i...  5.18 us
    ppermute x8, waiting for transfers between devices, moved(): return lax.ppermute(array, 'seq', [(j, j ^ number) for j in range(slots)])  4.66 us
    ppermute x4, starting transfers between devices, onward(): return lax.ppermute(array, ('seq', 'section'), pairs)  4.27 us
    ppermute x4, waiting for transfers between devices, onward(): return lax.ppermute(array, ('seq', 'section'), pairs)  3.96 us
  transfers between devices with their start and end apart: 12, of which 5 were waited for; matrix products, arithmetic and copies ran while one was open for 0% of the time, Pallas kernels for 12%

profile of v4, /device:TPU:0, one launch (start us, length us, event | category | flops | bytes accessed | tf_op | source)
XLA Modules:
  0.0 32.7 jit_solution(7927162995688272042)
XLA Ops:
  0.6 0.0 copy-start.1
  0.6 0.0 copy-start.4
  0.6 0.0 copy-start.5
  0.7 3.1 %collective-permute-start.2 = (bf16[4,3072]{1,0:T(4,128)(2,1)}, bf16[4,3072]{1,0:T(4,128)(2,1)S(1)}, u32[]{:S(2)}, u32[]{:S(2)}) collective-permute-start(bf16[4,3072]{1,0:T(4,128)(2,1)} %bitcast.20), channel_id=1, source_target_pairs={{0,4},{4,0},{8,12},{12,8},{1,5},{5,1},{9,13},{13,9},{2,6},{6,2},{1... | collective-permute-start | bytes 73736 | tf_op jit(solution)/shard_map/ppermute | solution.py:236
  3.8 2.6 %collective-permute-start.1 = (bf16[4,3072]{1,0:T(4,128)(2,1)}, bf16[4,3072]{1,0:T(4,128)(2,1)S(1)}, u32[]{:S(2)}, u32[]{:S(2)}) collective-permute-start(bf16[4,3072]{1,0:T(4,128)(2,1)} %bitcast.21), channel_id=1, source_target_pairs={{0,8},{4,12},{8,0},{12,4},{1,9},{5,13},{9,1},{13,5},{2,10},{6,14},... | collective-permute-start | bytes 73736 | tf_op jit(solution)/shard_map/ppermute | solution.py:236
  6.4 0.0 slice-start.2
  6.4 0.0 slice-start.3
  6.4 0.0 copy-start
  6.4 0.0 copy-start.2
  6.4 0.0 copy-start.3
  6.4 0.1 shard_map.96
  6.6 0.0 slice-start.4
  6.6 0.0 slice-start.5
  6.6 0.3 collective-permute-start
  6.9 0.2 shard_map.98
  7.1 0.0 slice-start
  7.1 1.7 %collective-permute-start.3 = (bf16[24,768]{1,0:T(8,128)(2,1)S(1)}, bf16[24,768]{1,0:T(8,128)(2,1)S(1)}, u32[]{:S(2)}, u32[]{:S(2)}) collective-permute-start(bf16[24,768]{1,0:T(8,128)(2,1)S(1)} %get-tuple-element.23), channel_id=1, source_target_pairs={{0,8},{4,12},{8,0},{12,4},{1,9},{5,13},{9,1},{13,5},{2,10},{6,14},... | collective-permute-start | bytes 110600 | tf_op jit(solution)/shard_map/ppermute | solution.py:236
  8.8 2.5 %collective-permute-start.4 = (bf16[24,768]{1,0:T(8,128)(2,1)S(1)}, bf16[24,768]{1,0:T(8,128)(2,1)S(1)}, u32[]{:S(2)}, u32[]{:S(2)}) collective-permute-start(bf16[24,768]{1,0:T(8,128)(2,1)S(1)} %get-tuple-element.24), channel_id=1, source_target_pairs={{0,4},{4,0},{8,12},{12,8},{1,5},{5,1},{9,13},{13,9},{2,6},{6,2},{1... | collective-permute-start | bytes 110600 | tf_op jit(solution)/shard_map/ppermute | solution.py:236
  11.3 0.0 collective-permute-done.2.refs_2_
  11.3 0.0 collective-permute-done.1.refs_1_
  11.3 1.5 %collective-permute-done.refs_0_ = bf16[40,768]{1,0:T(8,128)(2,1)S(1)} collective-permute-done((bf16[40,768]{1,0:T(8,128)(2,1)S(1)}, bf16[40,768]{1,0:T(8,128)(2,1)S(1)}, u32[]{:S(2)}, u32[]{:S(2)}) %collective-permute-start) | collective-permute-done | bytes 61472 | tf_op jit(solution)/shard_map/ppermute | solution.py:236
  12.8 0.0 slice-done.2
  12.8 0.0 copy-done
  12.8 0.0 slice-start.1
  12.8 2.1 %shard_map.97 = (bf16[16,768]{1,0:T(8,128)(2,1)S(1)}, bf16[16,768]{1,0:T(8,128)(2,1)S(1)}, bf16[16,768]{1,0:T(8,128)(2,1)S(1)}, bf16[16,768]{1,0:T(8,128)(2,1)S(1)}, f32[1,768]{1,0:T(1,128)S(1)}) custom-call(s32[1,4]{1,0:T(1,128)S(1)} %bitcast.26, f32[3,4,3072]{2,1,0:T(4,128)S(1)} %bitcast.19, f32[2,128]{1,0:T(2,128)S(1)} %bitcast.25, ...), custom_call_target="tpu_custom_call" | custom-call | flops 2000000000 | bytes 1048576 | tf_op jit(solution)/shard_map/pallas_call | solution.py:208
  15.0 0.0 collective-permute-done.3.refs_1_
  15.0 0.0 collective-permute-done.4.refs_2_
  15.0 0.4 %shard_map.99 = (bf16[24,768]{1,0:T(8,128)(2,1)S(1)}, bf16[24,768]{1,0:T(8,128)(2,1)S(1)}, bf16[24,768]{1,0:T(8,128)(2,1)S(1)}, bf16[24,768]{1,0:T(8,128)(2,1)S(1)}) custom-call(bf16[16,768]{1,0:T(8,128)(2,1)S(1)} %get-tuple-element.20.q_ref, bf16[16,768]{1,0:T(8,128)(2,1)S(1)} %get-tuple-element.21.k_ref, bf16[16,768]{1,0:T(8,128)(2,1)S(1)} %get-tuple-element.22.v_ref, ...), custom_call_target="tpu_custom_call" | custom-call | flops 2000000000 | bytes 1048576 | tf_op jit(solution)/shard_map/pallas_call | solution.py:208
  15.4 0.6 %collective-permute-start.6 = (bf16[24,768]{1,0:T(8,128)(2,1)S(1)}, bf16[24,768]{1,0:T(8,128)(2,1)S(1)}, u32[]{:S(2)}, u32[]{:S(2)}) collective-permute-start(bf16[24,768]{1,0:T(8,128)(2,1)S(1)} %get-tuple-element.28), channel_id=1, source_target_pairs={{0,8},{4,12},{8,0},{12,4},{1,9},{5,13},{9,1},{13,5},{2,10},{6,14},... | collective-permute-start | bytes 110600 | tf_op jit(solution)/shard_map/ppermute | solution.py:236
  16.1 2.9 %collective-permute-start.5 = (bf16[24,768]{1,0:T(8,128)(2,1)S(1)}, bf16[24,768]{1,0:T(8,128)(2,1)S(1)}, u32[]{:S(2)}, u32[]{:S(2)}) collective-permute-start(bf16[24,768]{1,0:T(8,128)(2,1)S(1)} %get-tuple-element.26), channel_id=1, source_target_pairs={{0,12},{4,8},{8,4},{12,0},{1,13},{5,9},{9,5},{13,1},{2,14},{6,10},... | collective-permute-start | bytes 110600 | tf_op jit(solution)/shard_map/ppermute | solution.py:236
  18.9 0.1 collective-permute-start.7
  19.0 1.4 %collective-permute-done.6.refs_1_ = bf16[24,768]{1,0:T(8,128)(2,1)S(1)} collective-permute-done((bf16[24,768]{1,0:T(8,128)(2,1)S(1)}, bf16[24,768]{1,0:T(8,128)(2,1)S(1)}, u32[]{:S(2)}, u32[]{:S(2)}) %collective-permute-start.6) | collective-permute-done | bytes 36896 | tf_op jit(solution)/shard_map/ppermute | solution.py:236
  20.4 0.0 slice-done
  20.4 0.4 %shard_map.100.refs_1_ = f32[16,768]{1,0:T(8,128)S(1)} custom-call(bf16[3072,768]{1,0:T(8,128)(2,1)S(1)} %bitcast.13, bf16[24,768]{1,0:T(8,128)(2,1)S(1)} %get-tuple-element.27.refs_0_.refs_3_, bf16[24,768]{1,0:T(8,128)(2,1)S(1)} %collective-permute-done.6.refs_1_), custom_call_target="tpu_custom_call" | custom-call | flops 1000000000 | bytes 1048576 | tf_op jit(solution)/shard_map/pallas_call | solution.py:208
  20.8 1.0 %collective-permute-done.5.refs_0_ = bf16[24,768]{1,0:T(8,128)(2,1)S(1)} collective-permute-done((bf16[24,768]{1,0:T(8,128)(2,1)S(1)}, bf16[24,768]{1,0:T(8,128)(2,1)S(1)}, u32[]{:S(2)}, u32[]{:S(2)}) %collective-permute-start.5) | collective-permute-done | bytes 36896 | tf_op jit(solution)/shard_map/ppermute | solution.py:236
  21.8 0.3 shard_map.101.total_ref
  22.1 0.8 %collective-permute-done.7.attention_ref.refs_2_ = bf16[24,768]{1,0:T(8,128)(2,1)S(1)} collective-permute-done((bf16[24,768]{1,0:T(8,128)(2,1)S(1)}, bf16[24,768]{1,0:T(8,128)(2,1)S(1)}, u32[]{:S(2)}, u32[]{:S(2)}) %collective-permute-start.7) | collective-permute-done | bytes 36896 | tf_op jit(solution)/shard_map/ppermute | solution.py:236
  22.9 0.3 shard_map.102
  23.2 0.1 collective-permute-start.8
  23.2 3.1 %collective-permute-start.9 = (bf16[4,768]{1,0:T(4,128)(2,1)S(1)}, bf16[4,768]{1,0:T(4,128)(2,1)S(1)}, u32[]{:S(2)}, u32[]{:S(2)}) collective-permute-start(bf16[4,768]{1,0:T(4,128)(2,1)S(1)} %get-tuple-element.31), channel_id=1, source_target_pairs={{0,1},{1,2},{2,3},{3,0},{4,5},{5,6},{6,7},{7,4},{8,9},{9,14},{10,1... | collective-permute-start | bytes 18440 | tf_op jit(solution)/shard_map/ppermute | solution.py:245
  26.4 0.0 collective-permute-start.10
  26.4 1.1 %collective-permute-start.11 = (bf16[4,768]{1,0:T(4,128)(2,1)S(1)}, bf16[4,768]{1,0:T(4,128)(2,1)S(1)}, u32[]{:S(2)}, u32[]{:S(2)}) collective-permute-start(bf16[4,768]{1,0:T(4,128)(2,1)S(1)} %get-tuple-element.33), channel_id=1, source_target_pairs={{0,9},{1,6},{2,11},{3,4},{4,13},{5,10},{6,15},{7,8},{8,5},{9,2},{1... | collective-permute-start | bytes 18440 | tf_op jit(solution)/shard_map/ppermute | solution.py:245
  27.5 0.7 %shard_map.104 = bf16[1,4,2,3072]{3,2,1,0:T(2,128)(2,1)} custom-call(bf16[24,768]{1,0:T(8,128)(2,1)S(1)} %collective-permute-done.5.refs_0_, bf16[24,768]{1,0:T(8,128)(2,1)S(1)} %collective-permute-done.6.refs_1_, bf16[24,768]{1,0:T(8,128)(2,1)S(1)} %collective-permute-done.7.attention_ref.refs_2_, bf16[24,768]{1,0:T(8,128)(2,1)S(1)} %get-tuple-element.27.refs_0_.refs_3_), custom_call_target="tpu_custom_call" | custom-call | flops 1000000000 | bytes 1048576 | tf_op jit(solution)/shard_map/pallas_call | solution.py:208
  28.2 0.0 collective-permute-done.8.refs_0_
  28.2 0.0 collective-permute-done.9.refs_1_
  28.2 3.9 %collective-permute-done.10.refs_2_ = bf16[4,768]{1,0:T(4,128)(2,1)S(1)} collective-permute-done((bf16[4,768]{1,0:T(4,128)(2,1)S(1)}, bf16[4,768]{1,0:T(4,128)(2,1)S(1)}, u32[]{:S(2)}, u32[]{:S(2)}) %collective-permute-start.10) | collective-permute-done | bytes 6176 | tf_op jit(solution)/shard_map/ppermute | solution.py:245
  32.1 0.0 collective-permute-done.11.refs_3_
  32.1 0.6 %shard_map.103 = bf16[1,4,3072]{2,1,0:T(4,128)(2,1)} custom-call(bf16[4,768]{1,0:T(4,128)(2,1)S(1)} %collective-permute-done.8.refs_0_, bf16[4,768]{1,0:T(4,128)(2,1)S(1)} %collective-permute-done.9.refs_1_, bf16[4,768]{1,0:T(4,128)(2,1)S(1)} %collective-permute-done.10.refs_2_, bf16[4,768]{1,0:T(4,128)(2,1)S(1)} %collective-permute-done.11.refs_3_), custom_call_target="tpu_custom_call" | custom-call | flops 1000000000 | bytes 1048576 | tf_op jit(solution)/shard_map/pallas_call | solution.py:208
  (12 shorter events, 0.0 us)
Async XLA Ops:
  0.6 5.7 %copy-start.1 = (bf16[1,4,3072]{2,1,0:T(4,128)(2,1)S(1)}, bf16[1,4,3072]{2,1,0:T(4,128)(2,1)}, u32[]{:S(2)}) copy-start(bf16[1,4,3072]{2,1,0:T(4,128)(2,1)} %param.8) | copy-start | bytes 73732
  0.6 5.7 %copy-start.4 = (bf16[1,4,4,2,3072]{4,3,2,1,0:T(2,128)(2,1)S(1)}, bf16[1,4,4,2,3072]{4,3,2,1,0:T(2,128)(2,1)}, u32[]{:S(2)}) copy-start(bf16[1,4,4,2,3072]{4,3,2,1,0:T(2,128)(2,1)} %cache_ref.3) | copy-start | bytes 589828
  0.6 5.7 %copy-start.5 = (s32[4]{0:T(128)S(1)}, s32[4]{0:T(128)}, u32[]{:S(2)}) copy-start(s32[4]{0:T(128)} %param.14) | copy-start | bytes 52
  0.7 10.7 %collective-permute-start.2 = (bf16[4,3072]{1,0:T(4,128)(2,1)}, bf16[4,3072]{1,0:T(4,128)(2,1)S(1)}, u32[]{:S(2)}, u32[]{:S(2)}) collective-permute-start(bf16[4,3072]{1,0:T(4,128)(2,1)} %bitcast.20), channel_id=1, source_target_pairs={{0,4},{4,0},{8,12},{12,8},{1,5},{5,1},{9,13},{13,9},{2,6},{6,2},{1... | collective-permute-start | bytes 73736 | tf_op jit(solution)/shard_map/ppermute | solution.py:236
  3.8 7.5 %collective-permute-start.1 = (bf16[4,3072]{1,0:T(4,128)(2,1)}, bf16[4,3072]{1,0:T(4,128)(2,1)S(1)}, u32[]{:S(2)}, u32[]{:S(2)}) collective-permute-start(bf16[4,3072]{1,0:T(4,128)(2,1)} %bitcast.21), channel_id=1, source_target_pairs={{0,8},{4,12},{8,0},{12,4},{1,9},{5,13},{9,1},{13,5},{2,10},{6,14},... | collective-permute-start | bytes 73736 | tf_op jit(solution)/shard_map/ppermute | solution.py:236
  6.4 6.4 %slice-start.2 = ((s8[14155776]{0:T(1024)(128)(4,1)}), s8[4194304]{0:T(1024)(128)(4,1)S(1)}, s32[]{:S(2)}) async-start(s8[14155776]{0:T(1024)(128)(4,1)} %bitcast.16), calls=%async_computation.2 | async-start | bytes 8388608
  6.4 6.4 %slice-start.3 = ((s8[14155776]{0:T(1024)(128)(4,1)}), s8[4194304]{0:T(1024)(128)(4,1)S(1)}, s32[]{:S(2)}) async-start(s8[14155776]{0:T(1024)(128)(4,1)} %bitcast.16), calls=%async_computation.3 | async-start | bytes 8388608
  6.4 6.4 %copy-start = (f32[1,4,3,3072]{3,1,2,0:T(4,128)S(1)}, f32[1,4,3,3072]{3,1,2,0:T(4,128)}, u32[]{:S(2)}) copy-start(f32[1,4,3,3072]{3,1,2,0:T(4,128)} %param.13) | copy-start | bytes 442372
  6.4 6.4 %copy-start.2 = (f32[1,2,128]{2,1,0:T(2,128)S(1)}, f32[1,2,128]{2,1,0:T(2,128)}, u32[]{:S(2)}) copy-start(f32[1,2,128]{2,1,0:T(2,128)} %param.12) | copy-start | bytes 3076
  6.4 6.4 %copy-start.3 = (s32[4]{0:T(128)S(1)}, s32[4]{0:T(128)}, u32[]{:S(2)}) copy-start(s32[4]{0:T(128)} %param.15) | copy-start | bytes 52
  6.6 6.2 %slice-start.4 = ((s8[14155776]{0:T(1024)(128)(4,1)}), s8[4194304]{0:T(1024)(128)(4,1)S(1)}, s32[]{:S(2)}) async-start(s8[14155776]{0:T(1024)(128)(4,1)} %bitcast.16), calls=%async_computation.4 | async-start | bytes 8388608
  6.6 6.2 %slice-start.5 = ((s8[14155776]{0:T(1024)(128)(4,1)}), s8[1572864]{0:T(1024)(128)(4,1)S(1)}, s32[]{:S(2)}) async-start(s8[14155776]{0:T(1024)(128)(4,1)} %bitcast.16), calls=%async_computation.5 | async-start | bytes 3145728
  6.6 6.2 %collective-permute-start = (bf16[40,768]{1,0:T(8,128)(2,1)S(1)}, bf16[40,768]{1,0:T(8,128)(2,1)S(1)}, u32[]{:S(2)}, u32[]{:S(2)}) collective-permute-start(bf16[40,768]{1,0:T(8,128)(2,1)S(1)} %shard_map.96), channel_id=1, source_target_pairs={{0,12},{4,8},{8,4},{12,0},{1,13},{5,9},{9,5},{13,1},{2,14},{6,10},... | collective-permute-start | bytes 184328 | tf_op jit(solution)/shard_map/ppermute | solution.py:236
  7.1 13.3 %slice-start = ((s8[4718592]{0:T(1024)(128)(4,1)}), s8[4194304]{0:T(1024)(128)(4,1)S(1)}, s32[]{:S(2)}) async-start(s8[4718592]{0:T(1024)(128)(4,1)} %bitcast.11), calls=%async_computation | async-start | bytes 8388608
  7.1 7.9 %collective-permute-start.3 = (bf16[24,768]{1,0:T(8,128)(2,1)S(1)}, bf16[24,768]{1,0:T(8,128)(2,1)S(1)}, u32[]{:S(2)}, u32[]{:S(2)}) collective-permute-start(bf16[24,768]{1,0:T(8,128)(2,1)S(1)} %get-tuple-element.23), channel_id=1, source_target_pairs={{0,8},{4,12},{8,0},{12,4},{1,9},{5,13},{9,1},{13,5},{2,10},{6,14},... | collective-permute-start | bytes 110600 | tf_op jit(solution)/shard_map/ppermute | solution.py:236
  8.8 6.2 %collective-permute-start.4 = (bf16[24,768]{1,0:T(8,128)(2,1)S(1)}, bf16[24,768]{1,0:T(8,128)(2,1)S(1)}, u32[]{:S(2)}, u32[]{:S(2)}) collective-permute-start(bf16[24,768]{1,0:T(8,128)(2,1)S(1)} %get-tuple-element.24), channel_id=1, source_target_pairs={{0,4},{4,0},{8,12},{12,8},{1,5},{5,1},{9,13},{13,9},{2,6},{6,2},{1... | collective-permute-start | bytes 110600 | tf_op jit(solution)/shard_map/ppermute | solution.py:236
  12.8 7.5 %slice-start.1 = ((s8[4718592]{0:T(1024)(128)(4,1)}), s8[524288]{0:T(1024)(128)(4,1)S(1)}, s32[]{:S(2)}) async-start(s8[4718592]{0:T(1024)(128)(4,1)} %bitcast.11), calls=%async_computation.1 | async-start | bytes 1048576
  15.4 4.9 %collective-permute-start.6 = (bf16[24,768]{1,0:T(8,128)(2,1)S(1)}, bf16[24,768]{1,0:T(8,128)(2,1)S(1)}, u32[]{:S(2)}, u32[]{:S(2)}) collective-permute-start(bf16[24,768]{1,0:T(8,128)(2,1)S(1)} %get-tuple-element.28), channel_id=1, source_target_pairs={{0,8},{4,12},{8,0},{12,4},{1,9},{5,13},{9,1},{13,5},{2,10},{6,14},... | collective-permute-start | bytes 110600 | tf_op jit(solution)/shard_map/ppermute | solution.py:236
  16.1 5.8 %collective-permute-start.5 = (bf16[24,768]{1,0:T(8,128)(2,1)S(1)}, bf16[24,768]{1,0:T(8,128)(2,1)S(1)}, u32[]{:S(2)}, u32[]{:S(2)}) collective-permute-start(bf16[24,768]{1,0:T(8,128)(2,1)S(1)} %get-tuple-element.26), channel_id=1, source_target_pairs={{0,12},{4,8},{8,4},{12,0},{1,13},{5,9},{9,5},{13,1},{2,14},{6,10},... | collective-permute-start | bytes 110600 | tf_op jit(solution)/shard_map/ppermute | solution.py:236
  18.9 4.0 %collective-permute-start.7 = (bf16[24,768]{1,0:T(8,128)(2,1)S(1)}, bf16[24,768]{1,0:T(8,128)(2,1)S(1)}, u32[]{:S(2)}, u32[]{:S(2)}) collective-permute-start(bf16[24,768]{1,0:T(8,128)(2,1)S(1)} %get-tuple-element.29), channel_id=1, source_target_pairs={{0,4},{4,0},{8,12},{12,8},{1,5},{5,1},{9,13},{13,9},{2,6},{6,2},{1... | collective-permute-start | bytes 110600 | tf_op jit(solution)/shard_map/ppermute | solution.py:236
  23.2 5.0 %collective-permute-start.8 = (bf16[4,768]{1,0:T(4,128)(2,1)S(1)}, bf16[4,768]{1,0:T(4,128)(2,1)S(1)}, u32[]{:S(2)}, u32[]{:S(2)}) collective-permute-start(bf16[4,768]{1,0:T(4,128)(2,1)S(1)} %get-tuple-element.30), channel_id=1, source_target_pairs={{0,13},{1,14},{2,15},{3,12},{4,9},{5,2},{6,11},{7,0},{8,1},{9,10},... | collective-permute-start | bytes 18440 | tf_op jit(solution)/shard_map/ppermute | solution.py:245
  23.2 4.9 %collective-permute-start.9 = (bf16[4,768]{1,0:T(4,128)(2,1)S(1)}, bf16[4,768]{1,0:T(4,128)(2,1)S(1)}, u32[]{:S(2)}, u32[]{:S(2)}) collective-permute-start(bf16[4,768]{1,0:T(4,128)(2,1)S(1)} %get-tuple-element.31), channel_id=1, source_target_pairs={{0,1},{1,2},{2,3},{3,0},{4,5},{5,6},{6,7},{7,4},{8,9},{9,14},{10,1... | collective-permute-start | bytes 18440 | tf_op jit(solution)/shard_map/ppermute | solution.py:245
  26.4 5.8 %collective-permute-start.10 = (bf16[4,768]{1,0:T(4,128)(2,1)S(1)}, bf16[4,768]{1,0:T(4,128)(2,1)S(1)}, u32[]{:S(2)}, u32[]{:S(2)}) collective-permute-start(bf16[4,768]{1,0:T(4,128)(2,1)S(1)} %get-tuple-element.32), channel_id=1, source_target_pairs={{0,5},{1,10},{2,7},{3,8},{4,1},{5,14},{6,3},{7,12},{8,13},{9,6},{1... | collective-permute-start | bytes 18440 | tf_op jit(solution)/shard_map/ppermute | solution.py:245
  26.4 5.8 %collective-permute-start.11 = (bf16[4,768]{1,0:T(4,128)(2,1)S(1)}, bf16[4,768]{1,0:T(4,128)(2,1)S(1)}, u32[]{:S(2)}, u32[]{:S(2)}) collective-permute-start(bf16[4,768]{1,0:T(4,128)(2,1)S(1)} %get-tuple-element.33), channel_id=1, source_target_pairs={{0,9},{1,6},{2,11},{3,4},{4,13},{5,10},{6,15},{7,8},{8,5},{9,2},{1... | collective-permute-start | bytes 18440 | tf_op jit(solution)/shard_map/ppermute | solution.py:245
